TPU v7x, 32 devices: a whole 2x2x4 slice. The times are simulated.
32 devices in a mesh: wshard: 4 (over y, x), ctx: 2 (over core), tp: 4 (over z).
Axes of the slice: x: 2, y: 2, z: 4, core: 2. Of those that a mesh axis runs over, the one named last changes fastest.
Arguments:
- tokens: bfloat16 [4, 2048, 768], P('wshard', 'ctx'), may hold values from -6 to 6
- lengths: int32 [4], P('wshard'), may hold values from 512 to 2048, as said below
- qkv_weight: bfloat16 [768, 3, 768], P('wshard', None, 'tp'), may hold values from -0.21875 to 0.21875
- qv_bias: float32 [2, 768], P(None, 'tp'), may hold values from -3 to 3
- out_weight: bfloat16 [768, 768], P('wshard', 'tp'), may hold values from -0.75 to 0.75
- out_bias: float32 [768], replicated, may hold values from -3 to 3
- ln1_gain: float32 [768], replicated, may hold values from 0.5 to 1.5
- ln1_bias: float32 [768], replicated, may hold values from -3 to 3
- gated_weight: bfloat16 [768, 2, 3072], P('wshard', None, 'tp'), may hold values from -0.21875 to 0.21875
- down_weight: bfloat16 [768, 3072], P('wshard', 'tp'), may hold values from -0.109375 to 0.109375
- down_bias: float32 [768], replicated, may hold values from -3 to 3
- ln2_gain: float32 [768], replicated, may hold values from 0.5 to 1.5
- ln2_bias: float32 [768], replicated, may hold values from -3 to 3
- cotangent: bfloat16 [4, 2048, 768], P('wshard', 'ctx'), may hold values from -6 to 6
Outputs:
- layer_output: bfloat16 [4, 2048, 768], P('wshard', 'ctx')
- input_grad: float32 [4, 2048, 768], P('wshard', 'ctx')
- qkv_grad: float32 [768, 3, 768], P('wshard', None, 'tp')
- qvbias_grad: float32 [2, 768], P(None, 'tp')
- outw_grad: float32 [768, 768], P('wshard', 'tp')
- outb_grad: float32 [768], replicated
- ln1g_grad: float32 [768], replicated
- ln1b_grad: float32 [768], replicated
- gated_grad: float32 [768, 2, 3072], P('wshard', None, 'tp')
- down_grad: float32 [768, 3072], P('wshard', 'tp')
- downb_grad: float32 [768], replicated
- ln2g_grad: float32 [768], replicated
- ln2b_grad: float32 [768], replicated
Inputs may be any that keep to these rules, and one draw needn't show every extreme that they name: Each sequence holds lengths[s] valid positions at its start; in every draw some sequence is full (2048) and some has exactly 512.
All inputs are finite; a program needn't handle non-finite values.
Results may differ from a plain program's by a relative error of at most 0.014.
The roundings to bfloat16 on the way count: a program that leaves them out, or rounds other values in their place, can miss the bound.
Values may be sent and summed in bfloat16 or wider, within the bound.
No kernel may reach another device: no remote copies, remote signals or barrier semaphores. Data moves between devices by JAX's collectives and lax.ppermute only.
A program may use at most 128 MiB of HBM per device.

v0:
```python
import jax
import jax.numpy as jnp
from jax import lax
from jax.sharding import PartitionSpec as P

HEADS = 12
DH = 64


norm_eps = 1e-05


def layer_norm(inputs, norm_gain, norm_shift):
    center = inputs - jnp.mean(inputs, axis=-1, keepdims=True)
    spread = jnp.mean(center * center, axis=-1, keepdims=True)
    return center * lax.rsqrt(spread + norm_eps) * norm_gain + norm_shift


def gated_unit(gate_part, up_part):
    return jax.nn.gelu(gate_part, approximate=False) * up_part


def times_transposed(left, right):
    return lax.dot_general(
        left, right, (((1,), (1,)), ((), ())), preferred_element_type=jnp.float32
    )


def first_transposed(left, right):
    return lax.dot_general(
        left, right, (((0,), (0,)), ((), ())), preferred_element_type=jnp.float32
    )


def alibi_scores(queries, key_block, length, query_start, slopes):
    raw_scores = jnp.einsum(
        "qhe,khe->hqk", queries, key_block, preferred_element_type=jnp.float32
    ) * DH ** (-0.5)
    query_pos = query_start + jnp.arange(queries.shape[0], dtype=jnp.int32)
    key_pos = jnp.arange(key_block.shape[0], dtype=jnp.int32)
    distance = jnp.abs(query_pos[:, None] - key_pos[None, :]).astype(jnp.float32)
    biased = raw_scores - slopes[:, None, None] * distance[None, :, :]
    return jnp.where((key_pos < length)[None, None, :], biased, -1e30)


def local(
    tokens,
    lengths,
    qkv_weight,
    qv_bias,
    out_weight,
    out_bias,
    ln1_gain,
    ln1_bias,
    gated_weight,
    down_weight,
    down_bias,
    ln2_gain,
    ln2_bias,
    cotangent,
):
    seq_dev, local_len, model_width = tokens.shape
    row_count = seq_dev * local_len
    part_width = qv_bias.shape[1]
    heads_local = part_width // DH
    ff_local = gated_weight.shape[2]
    shard_rows = qkv_weight.shape[0]
    tp_place = lax.axis_index("tp")
    query_start = lax.axis_index("ctx") * local_len
    head_number = tp_place * heads_local + jnp.arange(heads_local, dtype=jnp.int32) + 1
    slopes = 2.0 ** (-8.0 * head_number.astype(jnp.float32) / HEADS)
    full_qkv, full_out, full_gated, full_down = (
        lax.all_gather(qkv_weight, "wshard", axis=0, tiled=True),
        lax.all_gather(out_weight, "wshard", axis=0, tiled=True),
        lax.all_gather(gated_weight, "wshard", axis=0, tiled=True),
        lax.all_gather(down_weight, "wshard", axis=0, tiled=True),
    )
    token_rows = tokens.reshape(row_count, model_width)
    grad_rows = cotangent.reshape(row_count, model_width)
    projected = jnp.dot(
        token_rows,
        full_qkv.reshape(model_width, 3 * part_width),
        preferred_element_type=jnp.float32,
    ).reshape(row_count, 3, part_width)
    queries = (projected[:, 0] + qv_bias[0]).astype(jnp.bfloat16)
    keys_own = projected[:, 1].astype(jnp.bfloat16)
    values_own = (projected[:, 2] + qv_bias[1]).astype(jnp.bfloat16)
    keys_all, values_all = (
        lax.all_gather(keys_own.reshape(seq_dev, local_len, part_width), "ctx", axis=1, tiled=True),
        lax.all_gather(
            values_own.reshape(seq_dev, local_len, part_width), "ctx", axis=1, tiled=True
        ),
    )
    query_heads = queries.reshape(seq_dev, local_len, heads_local, DH)
    key_heads = keys_all.reshape(seq_dev, -1, heads_local, DH)
    value_heads = values_all.reshape(seq_dev, -1, heads_local, DH)

    def attend(entry):
        query_part, key_part, value_part, length = entry
        scores = alibi_scores(query_part, key_part, length, query_start, slopes)
        row_top = jnp.max(scores, axis=-1, keepdims=True)
        exponent = jnp.exp(scores - row_top)
        row_total = jnp.sum(exponent, axis=-1, keepdims=True)
        weights_low = (exponent / row_total).astype(jnp.bfloat16)
        mixture = jnp.einsum(
            "hqk,khe->qhe", weights_low, value_part, preferred_element_type=jnp.float32
        )
        return (mixture.astype(jnp.bfloat16), (row_top + jnp.log(row_total))[:, :, 0])

    mixture, log_total = lax.map(attend, (query_heads, key_heads, value_heads, lengths))
    mixed_rows = mixture.reshape(row_count, part_width)
    attn_part = times_transposed(mixed_rows, full_out)
    own_grads = grad_rows.astype(jnp.float32)
    pre_first = token_rows.astype(jnp.float32) + (lax.psum(attn_part, "tp") + out_bias)
    norm_first = layer_norm(pre_first, ln1_gain, ln1_bias)
    norm_low = norm_first.astype(jnp.bfloat16)
    gate_up = jnp.dot(
        norm_low, full_gated.reshape(model_width, 2 * ff_local), preferred_element_type=jnp.float32
    ).reshape(row_count, 2, ff_local)
    activation = gated_unit(gate_up[:, 0], gate_up[:, 1]).astype(jnp.bfloat16)
    down_part = times_transposed(activation, full_down)
    pre_second = norm_first + (lax.psum(down_part, "tp") + down_bias)
    layer_rows = layer_norm(pre_second, ln2_gain, ln2_bias)
    unused_second, pull_second = jax.vjp(layer_norm, pre_second, ln2_gain, ln2_bias)
    grad_pre2, gain_two, shift_two = pull_second(own_grads)
    output_low = layer_rows.astype(jnp.bfloat16)
    grad_down = grad_pre2.astype(jnp.bfloat16)
    grad_act = jnp.dot(grad_down, full_down, preferred_element_type=jnp.float32)
    unused_unit, pull_unit = jax.vjp(gated_unit, gate_up[:, 0], gate_up[:, 1])
    grad_gate, grad_up = pull_unit(grad_act)
    grad_gated = (
        jnp.stack([grad_gate, grad_up], axis=1)
        .astype(jnp.bfloat16)
        .reshape(row_count, 2 * ff_local)
    )
    back_part = times_transposed(grad_gated, full_gated.reshape(model_width, 2 * ff_local))
    grad_norm1 = grad_pre2 + lax.psum(back_part, "tp")
    unused_first, pull_first = jax.vjp(layer_norm, pre_first, ln1_gain, ln1_bias)
    grad_pre1, gain_one, shift_one = pull_first(grad_norm1)
    grad_attn = grad_pre1.astype(jnp.bfloat16)
    grad_mixed = jnp.dot(grad_attn, full_out, preferred_element_type=jnp.float32).astype(
        jnp.bfloat16
    )
    grad_heads = grad_mixed.reshape(seq_dev, local_len, heads_local, DH)

    def attend_back(entry):
        query_part, key_part, value_part, length, log_part, grad_part = entry
        scores = alibi_scores(query_part, key_part, length, query_start, slopes)
        attention = jnp.exp(scores - log_part[:, :, None])
        grad_weights = jnp.einsum(
            "qhe,khe->hqk", grad_part, value_part, preferred_element_type=jnp.float32
        )
        row_dot = jnp.sum(grad_weights * attention, axis=-1, keepdims=True)
        grad_scores = (attention * (grad_weights - row_dot)).astype(jnp.bfloat16)
        grad_query = jnp.einsum(
            "hqk,khe->qhe", grad_scores, key_part, preferred_element_type=jnp.float32
        ) * DH ** (-0.5)
        grad_key = jnp.einsum(
            "hqk,qhe->khe", grad_scores, query_part, preferred_element_type=jnp.float32
        ) * DH ** (-0.5)
        grad_value = jnp.einsum(
            "hqk,qhe->khe",
            attention.astype(jnp.bfloat16),
            grad_part,
            preferred_element_type=jnp.float32,
        )
        return (grad_query.astype(jnp.bfloat16), grad_key, grad_value)

    grad_query, grad_key_all, grad_value_all = lax.map(
        attend_back, (query_heads, key_heads, value_heads, lengths, log_total, grad_heads)
    )
    grad_key, grad_value = (
        lax.psum_scatter(
            grad_key_all.reshape(seq_dev, -1, part_width), "ctx", scatter_dimension=1, tiled=True
        ),
        lax.psum_scatter(
            grad_value_all.reshape(seq_dev, -1, part_width), "ctx", scatter_dimension=1, tiled=True
        ),
    )
    query_low = grad_query.reshape(row_count, part_width)
    value_low = grad_value.reshape(row_count, part_width).astype(jnp.bfloat16)
    grad_proj = jnp.stack(
        [query_low, grad_key.reshape(row_count, part_width).astype(jnp.bfloat16), value_low], axis=1
    ).reshape(row_count, 3 * part_width)
    input_part = times_transposed(grad_proj, full_qkv.reshape(model_width, 3 * part_width))
    input_rows = grad_pre1 + lax.psum(input_part, "tp")
    shard_grads = lax.psum_scatter(
        jnp.concatenate(
            [
                first_transposed(token_rows, grad_proj),
                first_transposed(grad_attn, mixed_rows),
                first_transposed(norm_low, grad_gated),
                first_transposed(grad_down, activation),
            ],
            axis=1,
        ),
        "wshard",
        scatter_dimension=0,
        tiled=True,
    )
    shard_grads = lax.psum(shard_grads, "ctx")
    qkv_end = 3 * part_width
    out_end = qkv_end + part_width
    gated_end = out_end + 2 * ff_local
    qkv_grad = shard_grads[:, :qkv_end].reshape(shard_rows, 3, part_width)
    outw_grad = shard_grads[:, qkv_end:out_end]
    gated_grad = shard_grads[:, out_end:gated_end].reshape(shard_rows, 2, ff_local)
    down_grad = shard_grads[:, gated_end:]
    bias_terms = jnp.stack(
        [
            jnp.sum(query_low.astype(jnp.float32), axis=0),
            jnp.sum(value_low.astype(jnp.float32), axis=0),
        ],
        axis=0,
    )
    qvbias_grad, outb_grad, ln1g_grad, ln1b_grad, downb_grad, ln2g_grad, ln2b_grad = lax.psum(
        (
            bias_terms,
            jnp.sum(grad_pre1, axis=0),
            gain_one,
            shift_one,
            jnp.sum(grad_pre2, axis=0),
            gain_two,
            shift_two,
        ),
        ("wshard", "ctx"),
    )
    layer_output = output_low.reshape(seq_dev, local_len, model_width)
    input_grad = input_rows.reshape(seq_dev, local_len, model_width)
    return (
        layer_output,
        input_grad,
        qkv_grad,
        qvbias_grad,
        outw_grad,
        outb_grad,
        ln1g_grad,
        ln1b_grad,
        gated_grad,
        down_grad,
        downb_grad,
        ln2g_grad,
        ln2b_grad,
    )


def solution(mesh):
    return jax.shard_map(
        local,
        mesh=mesh,
        in_specs=(
            P("wshard", "ctx", None),
            P("wshard"),
            P("wshard", None, "tp"),
            P(None, "tp"),
            P("wshard", "tp"),
            P(),
            P(),
            P(),
            P("wshard", None, "tp"),
            P("wshard", "tp"),
            P(),
            P(),
            P(),
            P("wshard", "ctx", None),
        ),
        out_specs=(
            P("wshard", "ctx", None),
            P("wshard", "ctx", None),
            P("wshard", None, "tp"),
            P(None, "tp"),
            P("wshard", "tp"),
            P(),
            P(),
            P(),
            P("wshard", None, "tp"),
            P("wshard", "tp"),
            P(),
            P(),
            P(),
        ),
        check_vma=False,
    )
```

profile of v0, /device:TPU:0, one launch (start us, length us, event | category | flops | bytes accessed | tf_op | source)
XLA Modules:
  0.0 758.9 jit_solution(12784075745873838943)
XLA Ops:
  8.1 17.1 %all_gather.18 = bf16[768,3,192]{2,0,1:T(8,128)(2,1)S(1)} all-gather(bf16[192,3,192]{2,0,1:T(8,128)(2,1)} %param.16), channel_id=1, replica_groups=mesh['wshard'=4,'ctx'=2,'tp'=4] {'wshard'}, dimensions={0}, use_global_device_ids=true | all-gather | bytes 1105920 | tf_op jit(solution)/shard_map/all_gather | solution.py:73
  32.7 4.7 abs_convert_fusion
  41.7 8.5 %all_gather.21 = bf16[768,192]{1,0:T(8,128)(2,1)S(1)} all-gather(bf16[192,192]{1,0:T(8,128)(2,1)S(1)} %copy-done.34), channel_id=1, replica_groups=mesh['wshard'=4,'ctx'=2,'tp'=4] {'wshard'}, dimensions={0}, use_global_device_ids=true | all-gather | bytes 368640 | tf_op jit(solution)/shard_map/all_gather | solution.py:74
  50.2 13.7 %fusion.62 = (f32[3,1024]{1,0:T(4,128)S(1)}, f32[3,1024,2048]{2,1,0:T(8,128)}) fusion(f32[1024,2048]{1,0:T(8,128)} %abs_convert_fusion, f32[3]{0:T(128)S(1)} %multiply_power_fusion, bf16[2048,3,64]{0,2,1:T(8,128)(2,1)S(1)} %bitcast.198, f32[1024,3,64]{0,2,1:T(8,128)S(1)} %bitcast.196, f32[3,64]{1,0:T(4,128)S(1)} %add.174, ...), kind=kOutput, calls=%fused_computation.121 | convolution fusion | flops 837153792 | bytes 35142412 | tf_op jit(solution)/shard_map/while/body/eval_jaxpr/qhe,khe->hqk/dot_general | solution.py:36
  63.9 10.4 %fusion = f32[3,1024]{1,0:T(4,128)S(1)} fusion(f32[3,1024,2048]{2,1,0:T(8,128)} %get-tuple-element.136, f32[3,1024]{1,0:T(4,128)S(1)} %get-tuple-element.135), kind=kLoop, calls=%fused_computation.6 | loop fusion | flops 12579840 | bytes 25190400 | tf_op jit(solution)/shard_map/while/body/eval_jaxpr/reduce_sum | solution.py:103
  74.4 10.6 %fusion.45 = bf16[3,64,1024]{2,1,0:T(8,128)(2,1)S(1)} fusion(bf16[2048,3,64]{0,2,1:T(8,128)(2,1)S(1)} %bitcast.206, f32[3,1024,2048]{2,1,0:T(8,128)} %get-tuple-element.136, f32[3,1024]{1,0:T(4,128)S(1)} %fusion, f32[3,1024]{1,0:T(4,128)S(1)} %get-tuple-element.135), kind=kOutput, calls=%fused_computation.85 | convolution fusion | flops 824377344 | bytes 26370048 | tf_op jit(solution)/shard_map/while/body/eval_jaxpr/hqk,khe->qhe/dot_general | solution.py:105
  89.9 119.7 %all-reduce.7.cloned.1.call-done = f32[1024,768]{1,0:T(8,128)} async-done(((f32[1024,768]{1,0:T(8,128)}), f32[1024,768]{1,0:T(8,128)}) %all-reduce.7.cloned.1.call-update) | async-done | bytes 3145744 | tf_op jit(solution)/shard_map/psum | solution.py:114
  213.0 4.3 copy.35
  217.3 4.6 fusion.33
  224.6 7.8 %multiply_convert_fusion.1 = (bf16[1024,768]{0,1:T(8,128)(2,1)}, f32[1024,768]{0,1:T(8,128)}) fusion(f32[1024,2,768]{0,2,1:T(8,128)S(1)} %fusion.33), kind=kLoop, calls=%fused_computation.46 | loop fusion | flops 51904512 | bytes 11010048 | tf_op jit(solution)/shard_map/convert_element_type | solution.py:120
  232.5 4.9 fusion.64
  237.7 119.9 %all-reduce.9.cloned.1.call-done = f32[1024,768]{1,0:T(8,128)} async-done(((f32[1024,768]{1,0:T(8,128)}), f32[1024,768]{1,0:T(8,128)}) %all-reduce.9.cloned.1.call-update) | async-done | bytes 3145744 | tf_op jit(solution)/shard_map/psum | solution.py:122
  372.1 4.4 convolution_bitcast_fusion.1
  377.1 119.7 %all-reduce.11.cloned.1.call-done = f32[1024,768]{1,0:T(8,128)} async-done(((f32[1024,768]{1,0:T(8,128)}), f32[1024,768]{1,0:T(8,128)}) %all-reduce.11.cloned.1.call-update) | async-done | bytes 3145744 | tf_op jit(solution)/shard_map/psum | solution.py:137
  496.8 4.4 multiply_reduce_fusion.1
  505.1 16.4 %multiply_reduce_fusion = (f32[3,1024]{1,0:T(4,128)}, f32[3,1024,2048]{2,1,0:T(8,128)}) fusion(f32[3,1024,2048]{2,1,0:T(8,128)} %get-tuple-element.136, f32[3,1024]{1,0:T(4,128)S(1)} %log_add_fusion, bf16[1024,3,64]{0,2,1:T(8,128)(2,1)S(1)} %bitcast.203, bf16[2048,3,64]{0,2,1:T(8,128)(2,1)} %bitcast.207), kind=kOutput, calls=%fused_computation.1 | convolution fusion | flops 824177664 | bytes 51535872 | tf_op jit(solution)/shard_map/while/body/eval_jaxpr/qhe,khe->hqk/dot_general | solution.py:150
  521.5 17.0 %multiply_convert_fusion = bf16[3,1024,2048]{2,1,0:T(8,128)(2,1)S(1)} fusion(f32[3,1024,2048]{2,1,0:T(8,128)} %get-tuple-element.138, f32[3,1024,2048]{2,1,0:T(8,128)} %get-tuple-element.136, f32[3,1024]{1,0:T(4,128)} %get-tuple-element.137, f32[3,1024]{1,0:T(4,128)S(1)} %log_add_fusion), kind=kLoop, calls=%fused_computation | loop fusion | flops 25165824 | bytes 62939136 | tf_op jit(solution)/shard_map/while/body/eval_jaxpr/convert_element_type | solution.py:154
  538.6 4.0 convolution_multiply_fusion
  543.7 12.2 %fusion.2 = f32[3,64,2048]{2,1,0:T(8,128)} fusion(bf16[1024,3,64]{0,2,1:T(8,128)(2,1)S(1)} %bitcast.204, f32[3,1024,2048]{2,1,0:T(8,128)} %get-tuple-element.136, f32[3,1024]{1,0:T(4,128)S(1)} %log_add_fusion), kind=kOutput, calls=%fused_computation.8 | convolution fusion | flops 817889280 | bytes 27144192 | tf_op jit(solution)/shard_map/while/body/eval_jaxpr/hqk,qhe->khe/dot_general | solution.py:161
  562.6 5.1 fusion.54
  580.6 9.9 %concatenate.3 = f32[768,3072]{1,0:T(8,128)} concatenate(f32[768,576]{1,0:T(8,128)S(1)} %copy.37, f32[768,192]{1,0:T(8,128)S(1)} %fusion.53, f32[768,1536]{1,0:T(8,128)} %fusion.54, f32[768,768]{1,0:T(8,128)} %fusion.51), dimensions={1} | concatenate | bytes 18874368 | tf_op jit(solution)/shard_map/concatenate | solution.py:188
  595.1 89.0 %reduce-scatter.8.cloned.1.call-done = f32[192,3072]{1,0:T(8,128)} async-done(((f32[768,3072]{1,0:T(8,128)}), f32[192,3072]{1,0:T(8,128)}) %reduce-scatter.8.cloned.1.call-update) | async-done | bytes 2359312 | tf_op jit(solution)/shard_map/reduce_scatter | solution.py:187
  686.0 28.9 %all-reduce.13.cloned.1.call-done = f32[1024,768]{1,0:T(8,128)} async-done(((f32[1024,768]{1,0:T(8,128)}), f32[1024,768]{1,0:T(8,128)}) %all-reduce.13.cloned.1.call-update) | async-done | bytes 3145744 | tf_op jit(solution)/shard_map/psum | solution.py:186
  718.9 24.4 %all-reduce = (f32[2,192]{1,0:T(2,128)}, f32[768]{0:T(1024)}, f32[768]{0:T(1024)}, f32[768]{0:T(1024)}, f32[768]{0:T(1024)}, /*index=5*/f32[768]{0:T(1024)}, f32[768]{0:T(1024)}) all-reduce(f32[2,192]{1,0:T(2,128)S(1)} %pad_maximum_fusion.1, ...), channel_id=1, replica_groups=mesh['wshard'=4,'ctx'=2,'tp'=4] {'wshard','ctx'}, use_global_device_ids=true, to_apply=%region_21.22 | all-reduce | flops 4992 | bytes 39936 | tf_op jit(solution)/shard_map/psum | solution.py:216
  (202 shorter events, 80.0 us)
Async XLA Ops:
  8.0 18.5 %copy-start.22 = (bf16[1,1024,768]{2,1,0:T(8,128)(2,1)S(1)}, bf16[1,1024,768]{2,1,0:T(8,128)(2,1)}, u32[]{:S(2)}) copy-start(bf16[1,1024,768]{2,1,0:T(8,128)(2,1)} %param.14) | copy-start | bytes 4718596
  8.0 201.6 %all-reduce.7.cloned.1.call-start = ((), (), s32[]{:S(2)}) async-start(), calls=%async_computation.3 | async-start | bytes 6291456 | tf_op jit(solution)/shard_map/psum | solution.py:114
  30.3 19.9 %copy-start.4 = (f32[1024,1,192]{0,2,1:T(8,128)}, f32[1024,1,192]{0,2,1:T(8,128)S(1)}, u32[]{:S(2)}) copy-start(f32[1024,1,192]{0,2,1:T(8,128)S(1)} %slice.48) | copy-start | bytes 2359300
  41.7 32.7 %copy-start.17 = (bf16[1,2048,192]{1,2,0:T(8,128)(2,1)}, bf16[1,2048,192]{1,2,0:T(8,128)(2,1)S(1)}, u32[]{:S(2)}) copy-start(bf16[1,2048,192]{1,2,0:T(8,128)(2,1)S(1)} %all_gather.19) | copy-start | bytes 2359300
  50.2 34.8 %copy-start.14 = (bf16[768,192]{1,0:T(8,128)(2,1)}, bf16[768,192]{1,0:T(8,128)(2,1)S(1)}, u32[]{:S(2)}) copy-start(bf16[768,192]{1,0:T(8,128)(2,1)S(1)} %all_gather.21) | copy-start | bytes 884740
  88.0 121.6 %copy-start.48 = (f32[768]{0:T(1024)S(1)}, f32[768]{0:T(1024)}, u32[]{:S(2)}) copy-start(f32[768]{0:T(1024)} %param.19) | copy-start | bytes 9220
  88.1 124.9 %all-gather.4.cloned.1.call-start = ((), (), s32[]{:S(2)}) async-start(), calls=%async_computation.4 | async-start | bytes 2949120 | tf_op jit(solution)/shard_map/all_gather | solution.py:75
  89.0 143.4 %all-gather.6.cloned.1.call-start = ((), (), s32[]{:S(2)}) async-start(), calls=%async_computation.5 | async-start | bytes 1474560 | tf_op jit(solution)/shard_map/all_gather | solution.py:76
  89.6 268.0 %all-reduce.9.cloned.1.call-start = ((), (), s32[]{:S(2)}) async-start(), calls=%async_computation.6 | async-start | bytes 6291456 | tf_op jit(solution)/shard_map/psum | solution.py:122
  212.4 288.7 %copy-start.30 = (f32[1024]{0:T(1024)}, f32[1024]{0:T(1024)S(1)}, u32[]{:S(2)}) copy-start(f32[1024]{0:T(1024)S(1)} %broadcast_multiply_fusion.1) | copy-start | bytes 12292
  213.0 288.2 %copy-start.35 = (f32[1024]{0:T(1024)}, f32[1024]{0:T(1024)S(1)}, u32[]{:S(2)}) copy-start(f32[1024]{0:T(1024)S(1)} %fusion.49) | copy-start | bytes 12292
  237.4 120.2 %copy-start.49 = (f32[768]{0:T(1024)S(1)}, f32[768]{0:T(1024)}, u32[]{:S(2)}) copy-start(f32[768]{0:T(1024)} %param.24) | copy-start | bytes 9220
  237.4 259.4 %all-reduce.11.cloned.1.call-start = ((), (), s32[]{:S(2)}) async-start(), calls=%async_computation.7 | async-start | bytes 6291456 | tf_op jit(solution)/shard_map/psum | solution.py:137
  366.3 130.4 %copy-start.41 = (f32[1024]{0:T(1024)}, f32[1024]{0:T(1024)S(1)}, u32[]{:S(2)}) copy-start(f32[1024]{0:T(1024)S(1)} %negate_multiply_fusion.2) | copy-start | bytes 12292
  376.5 196.5 %reduce-scatter.4.cloned.1.call-start = ((), (), s32[]{:S(2)}) async-start(), calls=%async_computation.8 | async-start | bytes 2359296 | tf_op jit(solution)/shard_map/reduce_scatter | solution.py:173
  543.6 30.8 %reduce-scatter.6.cloned.1.call-start = ((), (), s32[]{:S(2)}) async-start(), calls=%async_computation.9 | async-start | bytes 2359296 | tf_op jit(solution)/shard_map/reduce_scatter | solution.py:176
  555.9 128.2 %reduce-scatter.8.cloned.1.call-start = ((), (), s32[]{:S(2)}) async-start(), calls=%async_computation.11 | async-start | bytes 11796480 | tf_op jit(solution)/shard_map/reduce_scatter | solution.py:187
  590.6 124.3 %all-reduce.13.cloned.1.call-start = ((), (), s32[]{:S(2)}) async-start(), calls=%async_computation.10 | async-start | bytes 6291456 | tf_op jit(solution)/shard_map/psum | solution.py:186
  595.0 119.9 %copy-start.3 = (f32[1024,768]{1,0:T(8,128)S(1)}, f32[1024,768]{1,0:T(8,128)}, u32[]{:S(2)}) copy-start(f32[1024,768]{1,0:T(8,128)} %copy-done.1) | copy-start | bytes 9437188
  595.1 148.3 %all-reduce.15.cloned.1.call-start = ((), (), s32[]{:S(2)}) async-start(), calls=%async_computation.12 | async-start | bytes 4718592 | tf_op jit(solution)/shard_map/psum | solution.py:201
  686.0 32.9 %copy-start.43 = (f32[768]{0:T(1024)S(1)}, f32[768]{0:T(1024)}, u32[]{:S(2)}) copy-start(f32[768]{0:T(1024)} %get-tuple-element.102) | copy-start | bytes 9220
  686.0 32.9 %copy-start.44 = (f32[768]{0:T(1024)S(1)}, f32[768]{0:T(1024)}, u32[]{:S(2)}) copy-start(f32[768]{0:T(1024)} %get-tuple-element.106) | copy-start | bytes 9220
  686.0 32.9 %copy-start.45 = (f32[768]{0:T(1024)S(1)}, f32[768]{0:T(1024)}, u32[]{:S(2)}) copy-start(f32[768]{0:T(1024)} %get-tuple-element.128) | copy-start | bytes 9220
  686.0 32.9 %copy-start.47 = (f32[768]{0:T(1024)S(1)}, f32[768]{0:T(1024)}, u32[]{:S(2)}) copy-start(f32[768]{0:T(1024)} %get-tuple-element.104) | copy-start | bytes 9220
  (48 other events, 217.6 us)
Sparse Core Ops, SparseCore 0:
  88.2 121.3 all-reduce.6
  237.5 120.0 all-reduce.8
  376.7 120.0 all-reduce.10
  595.2 119.6 all-reduce.12
  717.1 20.7 all-reduce.14
Sparse Core Ops, SparseCore 1:
  91.0 37.5 all-gather.3
  130.2 27.4 all-gather.5
  543.7 7.8 reduce-scatter.3
  556.0 8.0 reduce-scatter.5
  590.7 93.4 reduce-scatter.7
where the time goes:
time: 767 us; the launch traced here: 759 us
  waiting for transfers between devices  478 us (62%)
  matrix products  98 us (13%)
  other arithmetic  68.9 us (9%)
  blocking collectives  54.8 us (7%)
  local copies, waits for them, and re-layouts  40.6 us (5%)
  between operations  17 us (2%)
    psum x1, waiting for transfers between devices, local(): pre_second = norm_first + (lax.psum(down_part, 'tp') + down_bias)  120 us
    psum x1, waiting for transfers between devices, local(): lax.psum(attn_part, 'tp') + out_bias  120 us
    psum x1, waiting for transfers between devices, local(): grad_norm1 = grad_pre2 + lax.psum(back_part, 'tp')  120 us
    reduce_scatter x1, waiting for transfers between devices, local(): lax.psum_scatter(jnp.concatenate([first_transposed(token_rows, grad_proj)...  89 us
    psum x1, waiting for transfers between devices, local(): input_rows = grad_pre1 + lax.psum(input_part, 'tp')  28.9 us
    psum x1, blocking collectives, local(): lax.psum((bias_terms, jnp.sum(grad_pre1, axis=0), gain_one, shift_one, jn...  24.4 us
    all_gather x1, blocking collectives, local(): lax.all_gather(qkv_weight, 'wshard', axis=0, tiled=True)  17.1 us
    convert_element_type x1, other arithmetic, attend_back(): grad_scores = (attention * (grad_weights - row_dot)).astype(jnp.bfloat16)  17 us
  transfers between devices with their start and end apart: 10, of which 5 were waited for; matrix products, arithmetic and copies ran while one was open for 8% of the time, Pallas kernels for 0%

commit v1 on v0

v1 whole, which is shorter than its diff:
```python
import jax
import jax.numpy as jnp
from jax import lax
from jax.sharding import PartitionSpec as P

HEADS = 12
DH = 64
SCALE = DH ** (-0.5)
norm_eps = 1e-05
f32 = jnp.float32
bf16 = jnp.bfloat16


def layer_norm(inputs, norm_gain, norm_shift):
    center = inputs - jnp.mean(inputs, axis=-1, keepdims=True)
    spread = jnp.mean(center * center, axis=-1, keepdims=True)
    return center * lax.rsqrt(spread + norm_eps) * norm_gain + norm_shift


def gated_unit(gate_part, up_part):
    return jax.nn.gelu(gate_part, approximate=False) * up_part


def mm(left, right):
    return lax.dot_general(left, right, (((1,), (0,)), ((), ())), preferred_element_type=f32)


def mm_nt(left, right):
    return lax.dot_general(left, right, (((1,), (1,)), ((), ())), preferred_element_type=f32)


def mm_tn(left, right):
    return lax.dot_general(left, right, (((0,), (0,)), ((), ())), preferred_element_type=f32)


def log2_of(n):
    if n & (n - 1):
        raise ValueError("axis size")
    return n.bit_length() - 1


def swap(x, axis, mask, n):
    return lax.ppermute(x, axis, [(i, i ^ mask) for i in range(n)])


def pick(stacked, index):
    return lax.dynamic_index_in_dim(stacked, index, 0, keepdims=False)


def gather_wshard(piece, n_ws, n_ctx):
    stages = log2_of(n_ws)
    me, core = lax.axis_index("wshard"), lax.axis_index("ctx")
    held, masks = [piece], [[0] for _ in range(n_ctx)]
    for stage in range(stages):
        bit = [1 << ((stage + c) % stages) for c in range(n_ctx)]
        perm = [
            (w * n_ctx + c, (w ^ bit[c]) * n_ctx + c) for w in range(n_ws) for c in range(n_ctx)
        ]
        sent = held[0][None] if len(held) == 1 else jnp.stack(held)
        got = lax.ppermute(sent, ("wshard", "ctx"), perm)
        held = held + [got[i] for i in range(len(held))]
        masks = [m + [v ^ bit[c] for v in m] for c, m in enumerate(masks)]
    table = jnp.asarray(masks, jnp.int32)
    out = jnp.zeros((n_ws,) + piece.shape, piece.dtype)
    for p, part in enumerate(held):
        out = lax.dynamic_update_index_in_dim(out, part, me ^ table[core, p], 0)
    return out


def sum_all(x, mesh_shape):
    for axis in ("ctx", "tp", "wshard"):
        n = mesh_shape[axis]
        for stage in range(log2_of(n)):
            x = x + swap(x, axis, 1 << stage, n)
    return x


def tp_gather(x, t):
    far = swap(x, "tp", 2, 4)
    high = t // 2
    two = jnp.stack([jnp.where(high == 0, x, far), jnp.where(high == 0, far, x)])
    near = swap(two, "tp", 1, 4)
    low = t % 2
    both = jnp.stack([jnp.where(low == 0, two, near), jnp.where(low == 0, near, two)], axis=1)
    return both.reshape(4 * x.shape[0], x.shape[1])


def tp_scatter(x, t):
    rows, width = x.shape
    parts = x.reshape(2, 2, rows // 4, width)
    high, low = t // 2, t % 2
    away = lax.dynamic_index_in_dim(parts, 1 - low, 1, keepdims=False)
    home = lax.dynamic_index_in_dim(parts, low, 1, keepdims=False)
    home = home + swap(away.astype(bf16), "tp", 1, 4).astype(f32)
    far = pick(home, 1 - high)
    near = pick(home, high)
    return near + swap(far.astype(bf16), "tp", 2, 4).astype(f32)


def make_local(mesh):
    shape = mesh.shape
    n_ws, n_ctx, n_tp = shape["wshard"], shape["ctx"], shape["tp"]
    if n_tp != 4 or n_ctx != 2:
        raise ValueError("mesh")

    def local(
        tokens,
        lengths,
        qkv_weight,
        qv_bias,
        out_weight,
        out_bias,
        ln1_gain,
        ln1_bias,
        gated_weight,
        down_weight,
        down_bias,
        ln2_gain,
        ln2_bias,
        cotangent,
    ):
        seq_dev, length_here, width = tokens.shape
        if seq_dev != 1:
            raise ValueError("one sequence")
        part = qv_bias.shape[1]
        heads = part // DH
        rows = length_here // n_tp
        shard_rows = qkv_weight.shape[0]
        half_rows = shard_rows // n_ctx
        w, c, t = lax.axis_index("wshard"), lax.axis_index("ctx"), lax.axis_index("tp")
        x = tokens[0]
        length = lengths[0]
        head_number = t * heads + jnp.arange(heads, dtype=jnp.int32) + 1
        slopes = 2.0 ** (-8.0 * head_number.astype(f32) / HEADS)

        x_other = swap(x, "ctx", 1, n_ctx)
        qkv = gather_wshard(jnp.transpose(qkv_weight, (1, 0, 2)), n_ws, n_ctx)
        qkv = jnp.transpose(qkv, (1, 0, 2, 3)).reshape(3, width, part)

        out_blocks = lax.all_gather(out_weight, ("wshard", "tp"), axis=0, tiled=False)
        full_out = jnp.transpose(
            out_blocks.reshape(n_ws, n_tp, shard_rows, part), (0, 2, 1, 3)
        ).reshape(width, n_tp * part)

        def own_half(weight):
            return lax.dynamic_slice_in_dim(weight, c * half_rows, half_rows, 0)

        def gather_half(half):
            return lax.all_gather(half, ("wshard", "ctx"), axis=0, tiled=True)

        gated_half, down_half = own_half(gated_weight), own_half(down_weight)
        gated_far, down_far = swap(gated_half, "tp", 2, n_tp), swap(down_half, "tp", 2, n_tp)
        gated = [gather_half(gated_half), gather_half(gated_far)]
        down = [gather_half(down_half), gather_half(down_far)]

        q = (mm(x, qkv[0]) + qv_bias[0]).astype(bf16)
        keys = jnp.concatenate([mm(x, qkv[1]), mm(x_other, qkv[1])], axis=0).astype(bf16)
        values = (
            jnp.concatenate([mm(x, qkv[2]), mm(x_other, qkv[2])], axis=0) + qv_bias[1]
        ).astype(bf16)
        local_pos = jnp.arange(length_here, dtype=jnp.int32)
        q_pos = c * length_here + local_pos
        k_pos = jnp.concatenate([q_pos, (1 - c) * length_here + local_pos])
        qh = q.reshape(length_here, heads, DH)
        kh = keys.reshape(n_ctx * length_here, heads, DH)
        vh = values.reshape(n_ctx * length_here, heads, DH)

        def scores_of():
            raw = jnp.einsum("qhe,khe->hqk", qh, kh, preferred_element_type=f32) * SCALE
            distance = jnp.abs(q_pos[:, None] - k_pos[None, :]).astype(f32)
            biased = raw - slopes[:, None, None] * distance[None]
            return jnp.where((k_pos < length)[None, None, :], biased, -1e30)

        scores = scores_of()
        row_top = jnp.max(scores, axis=-1, keepdims=True)
        exponent = jnp.exp(scores - row_top)
        row_total = jnp.sum(exponent, axis=-1, keepdims=True)
        probs_low = (exponent / row_total).astype(bf16)
        mixed = jnp.einsum("hqk,khe->qhe", probs_low, vh, preferred_element_type=f32)
        mixed = mixed.astype(bf16).reshape(length_here, part)
        log_total = (row_top + jnp.log(row_total))[:, :, 0]

        mixed_rows = lax.all_to_all(mixed, "tp", 0, 1, tiled=True)
        x_rows = lax.dynamic_slice_in_dim(x, t * rows, rows, 0).astype(f32)
        cot_rows = lax.dynamic_slice_in_dim(cotangent[0], t * rows, rows, 0).astype(f32)
        pre1 = x_rows + (mm_nt(mixed_rows, full_out) + out_bias)
        norm1 = layer_norm(pre1, ln1_gain, ln1_bias)
        norm_low = norm1.astype(bf16)

        def neighbour(v):
            return swap(v, "tp", 1, n_tp)

        def forward(rows_low):
            kept, acts, total = [], [], None
            for g, d in zip(gated, down):
                gate, up = mm(rows_low, g[:, 0]), mm(rows_low, g[:, 1])
                act = gated_unit(gate, up).astype(bf16)
                kept.append((gate, up))
                acts.append(act)
                piece = mm_nt(act, d)
                total = piece if total is None else total + piece
            return kept, acts, total

        norm_near = neighbour(norm_low)
        kept_own, acts_own, down_own = forward(norm_low)
        kept_near, acts_near, down_near = forward(norm_near)
        down_sum = down_own + neighbour(down_near.astype(bf16)).astype(f32)
        pre2 = norm1 + (down_sum + down_bias)
        layer_rows, pull2 = jax.vjp(layer_norm, pre2, ln2_gain, ln2_bias)
        grad_pre2, ln2g, ln2b = pull2(cot_rows)
        output_rows = layer_rows.astype(bf16)
        grad_down = grad_pre2.astype(bf16)
        grad_near = neighbour(grad_down)

        def backward(grad_low, kept):
            pieces, total = [], None
            for g, d, (gate, up) in zip(gated, down, kept):
                grad_act = mm(grad_low, d)
                unused, pull = jax.vjp(gated_unit, gate, up)
                grad_gate, grad_up = pull(grad_act)
                grad_gate, grad_up = grad_gate.astype(bf16), grad_up.astype(bf16)
                pieces.append((grad_gate, grad_up))
                piece = mm_nt(grad_gate, g[:, 0]) + mm_nt(grad_up, g[:, 1])
                total = piece if total is None else total + piece
            return pieces, total

        ggu_own, back_own = backward(grad_down, kept_own)
        ggu_near, back_near = backward(grad_near, kept_near)
        back_got = neighbour(back_near.astype(bf16)).astype(f32)

        norm_both = jnp.concatenate([norm_low, norm_near], axis=0)
        grad_both = jnp.concatenate([grad_down, grad_near], axis=0)

        def reduce_rows(v):
            return lax.psum_scatter(v, ("wshard", "ctx"), scatter_dimension=0, tiled=True)

        ffn_shards = []
        for k in (1, 0):
            gg = jnp.concatenate([ggu_own[k][0], ggu_near[k][0]], axis=0)
            gu = jnp.concatenate([ggu_own[k][1], ggu_near[k][1]], axis=0)
            act = jnp.concatenate([acts_own[k], acts_near[k]], axis=0)
            whole = jnp.concatenate(
                [mm_tn(norm_both, gg), mm_tn(norm_both, gu), mm_tn(grad_both, act)], axis=1
            ).astype(bf16)
            ffn_shards.append(reduce_rows(whole))
        ffn_shard = ffn_shards[1].astype(f32) + swap(ffn_shards[0], "tp", 2, n_tp).astype(f32)

        grad_norm1 = grad_pre2 + (back_own + back_got)
        unused, pull1 = jax.vjp(layer_norm, pre1, ln1_gain, ln1_bias)
        grad_pre1, ln1g, ln1b = pull1(grad_norm1)
        grad_attn = grad_pre1.astype(bf16)
        grad_mixed_rows = mm(grad_attn, full_out).astype(bf16)
        grad_mixed = lax.all_to_all(grad_mixed_rows, "tp", 1, 0, tiled=True)
        outw_part = mm_tn(grad_attn, mixed_rows).astype(bf16)
        layer_output = tp_gather(output_rows, t)

        gh = grad_mixed.reshape(length_here, heads, DH)
        attention = jnp.exp(scores_of() - log_total[:, :, None])
        grad_weights = jnp.einsum("qhe,khe->hqk", gh, vh, preferred_element_type=f32)
        row_dot = jnp.sum(grad_weights * attention, axis=-1, keepdims=True)
        grad_scores = (attention * (grad_weights - row_dot)).astype(bf16)
        grad_q = jnp.einsum("hqk,khe->qhe", grad_scores, kh, preferred_element_type=f32) * SCALE
        grad_k = jnp.einsum("hqk,qhe->khe", grad_scores, qh, preferred_element_type=f32) * SCALE
        grad_v = jnp.einsum(
            "hqk,qhe->khe", attention.astype(bf16), gh, preferred_element_type=f32
        )
        grad_q = grad_q.astype(bf16).reshape(length_here, part)
        grad_kv = jnp.concatenate(
            [grad_k.reshape(-1, part), grad_v.reshape(-1, part)], axis=1
        )
        grad_kv = grad_kv[:length_here] + swap(grad_kv[length_here:], "ctx", 1, n_ctx)
        grad_kv = grad_kv.astype(bf16)
        grad_k, grad_v = grad_kv[:, :part], grad_kv[:, part:]

        input_part = mm_nt(grad_q, qkv[0]) + mm_nt(grad_k, qkv[1]) + mm_nt(grad_v, qkv[2])
        input_rows = grad_pre1 + tp_scatter(input_part, t)
        input_grad = tp_gather(input_rows.astype(bf16), t).astype(f32)

        grad_proj = jnp.concatenate([grad_q, grad_k, grad_v], axis=1)
        qkv_out = jnp.concatenate([mm_tn(x, grad_proj).astype(bf16), outw_part], axis=1)
        qkv_out = reduce_rows(qkv_out).astype(f32)
        qkv_shard, outw_shard = qkv_out[:, : 3 * part], qkv_out[:, 3 * part :]
        outw_shard = lax.psum_scatter(outw_shard, "tp", scatter_dimension=1, tiled=True)

        shard = jnp.concatenate([ffn_shard, qkv_shard, outw_shard], axis=1)
        other = swap(shard, "ctx", 1, n_ctx)
        shard = jnp.concatenate(
            [jnp.where(c == 0, shard, other), jnp.where(c == 0, other, shard)], axis=0
        )
        hidden = gated_weight.shape[2]
        gated_grad = shard[:, : 2 * hidden].reshape(shard_rows, 2, hidden)
        down_grad = shard[:, 2 * hidden : 3 * hidden]
        qkv_grad = shard[:, 3 * hidden : 3 * hidden + 3 * part].reshape(shard_rows, 3, part)
        outw_grad = shard[:, 3 * hidden + 3 * part :]

        bias_here = jnp.stack(
            [jnp.sum(grad_q.astype(f32), axis=0), jnp.sum(grad_v.astype(f32), axis=0)]
        )
        bias_slot = lax.dynamic_update_slice_in_dim(
            jnp.zeros((2, width), f32), bias_here, t * part, 1
        )
        sums = jnp.concatenate(
            [
                bias_slot,
                jnp.stack(
                    [jnp.sum(grad_pre1, axis=0), ln1g, ln1b, jnp.sum(grad_pre2, axis=0), ln2g, ln2b]
                ),
            ],
            axis=0,
        )
        sums = sum_all(sums, shape)
        qvbias_grad = lax.dynamic_slice_in_dim(sums[:2], t * part, part, 1)
        return (
            layer_output[None],
            input_grad[None],
            qkv_grad,
            qvbias_grad,
            outw_grad,
            sums[2],
            sums[3],
            sums[4],
            gated_grad,
            down_grad,
            sums[5],
            sums[6],
            sums[7],
        )

    return local


def solution(mesh):
    return jax.shard_map(
        make_local(mesh),
        mesh=mesh,
        in_specs=(
            P("wshard", "ctx", None),
            P("wshard"),
            P("wshard", None, "tp"),
            P(None, "tp"),
            P("wshard", "tp"),
            P(),
            P(),
            P(),
            P("wshard", None, "tp"),
            P("wshard", "tp"),
            P(),
            P(),
            P(),
            P("wshard", "ctx", None),
        ),
        out_specs=(
            P("wshard", "ctx", None),
            P("wshard", "ctx", None),
            P("wshard", None, "tp"),
            P(None, "tp"),
            P("wshard", "tp"),
            P(),
            P(),
            P(),
            P("wshard", None, "tp"),
            P("wshard", "tp"),
            P(),
            P(),
            P(),
        ),
        check_vma=False,
    )
```

time: 767 us -> 521 us (0.68)
  waiting for transfers between devices: 478 us -> 187 us
  blocking collectives: 54.8 us -> 0 us
  matrix products: 98 us -> 139 us
  local copies, waits for them, and re-layouts: 40.6 us -> 74.1 us
  starting transfers between devices: 1.53 us -> 33.2 us
  other arithmetic: 68.9 us -> 58.8 us
    psum x5 -> x0, waiting for transfers between devices: 388 us -> none  [the longest x1 120 us: local(): pre_second = norm_first + (lax.psum(down_part, 'tp') + down_bias)]
    ppermute x0 -> x23, waiting for transfers between devices: none -> 119 us  [the longest x21 115 us: swap(): return lax.ppermute(x, axis, [(i, i ^ mask) for i in range(n)])]
    reduce_scatter x3 -> x2, waiting for transfers between devices: 89.1 us -> 19.4 us  [the longest x1 19.4 us: local(): lax.psum_scatter(outw_shard, 'tp', scatter_dimension=1, tiled=True)]
    all_gather x2 -> x5, waiting for transfers between devices: 0.03 us -> 47.7 us  [the longest x4 47.7 us: gather_half(): return lax.all_gather(half, ('wshard', 'ctx'), axis=0, tiled=True)]
    dot_general x18 -> x48, matrix products: 98 us -> 139 us  [the longest x18 40.2 us: mm(): lax.dot_general(left, right, (((1,), (0,)), ((), ())), preferred_element_...]
    all_gather x4 -> x0, blocking collectives: 30.4 us -> none  [the longest x1 17.1 us: local(): lax.all_gather(qkv_weight, 'wshard', axis=0, tiled=True)]
    unnamed x122 -> x189, local copies, waits for them, and re-layouts: 16 us -> 44.4 us
    ppermute x0 -> x23, starting transfers between devices: none -> 25.2 us  [the longest x21 22.1 us: swap(): return lax.ppermute(x, axis, [(i, i ^ mask) for i in range(n)])]
  transfers between devices with their start and end apart: 10 -> 34, of which waited for: 5 -> 18; matrix products, arithmetic and copies ran while one was open for 8% -> 44% of each run, Pallas kernels for 0% -> 0%
where the time goes in v1:
time: 521 us; the launch traced here: 511 us
  waiting for transfers between devices  187 us (36%)
  matrix products  139 us (27%)
  local copies, waits for them, and re-layouts  74.1 us (14%)
  other arithmetic  58.8 us (11%)
  starting transfers between devices  33.2 us (6%)
  between operations  19 us (4%)
    ppermute x21, waiting for transfers between devices, swap(): return lax.ppermute(x, axis, [(i, i ^ mask) for i in range(n)])  115 us
    all_gather x4, waiting for transfers between devices, gather_half(): return lax.all_gather(half, ('wshard', 'ctx'), axis=0, tiled=True)  47.7 us
    unnamed x189, local copies, waits for them, and re-layouts  44.4 us
    dot_general x18, matrix products, mm(): lax.dot_general(left, right, (((1,), (0,)), ((), ())), preferred_element_...  40.2 us
    ppermute x21, starting transfers between devices, swap(): return lax.ppermute(x, axis, [(i, i ^ mask) for i in range(n)])  22.1 us
    dot_general x16, matrix products, mm_nt(): lax.dot_general(left, right, (((1,), (1,)), ((), ())), preferred_element_...  21.7 us
    dot_general x1, matrix products, local(): jnp.einsum('qhe,khe->hqk', gh, vh, preferred_element_type=f32)  20 us
    reduce_scatter x1, waiting for transfers between devices, local(): lax.psum_scatter(outw_shard, 'tp', scatter_dimension=1, tiled=True)  19.4 us
  transfers between devices with their start and end apart: 34, of which 18 were waited for; matrix products, arithmetic and copies ran while one was open for 44% of the time, Pallas kernels for 0%

profile of v1, /device:TPU:0, one launch (start us, length us, event | category | flops | bytes accessed | tf_op | source)
XLA Modules:
  0.0 510.7 jit_solution(3624467234423836464)
XLA Ops:
  18.4 4.7 abs_convert_fusion
  42.4 13.6 %fusion.125 = (f32[3,1024]{1,0:T(4,128)S(1)}, f32[3,1024,2048]{2,1,0:T(8,128)}) fusion(f32[1024,2048]{1,0:T(8,128)} %abs_convert_fusion, f32[3]{0:T(128)S(1)} %multiply_power_fusion, bf16[1024,3,64]{0,2,1:T(8,128)(2,1)S(1)} %bitcast.219, bf16[1024,3,64]{0,2,1:T(8,128)(2,1)S(1)} %bitcast.233, bf16[1024,3,64]{0,2,1:T(8,128)(2,1)S(1)} %bitcast.231, ...), kind=kOutput, calls=%fused_computation.289 | convolution fusion | flops 838333440 | bytes 34748428 | tf_op jit(solution)/shard_map/qhe,khe->hqk/dot_general | solution.py:169
  56.0 10.6 %fusion = f32[3,1024]{1,0:T(4,128)S(1)} fusion(f32[3,1024,2048]{2,1,0:T(8,128)} %get-tuple-element.108, f32[3,1024]{1,0:T(4,128)S(1)} %get-tuple-element.107), kind=kLoop, calls=%fused_computation.6 | loop fusion | flops 12579840 | bytes 25190400 | tf_op jit(solution)/shard_map/reduce_sum | solution.py:177
  69.6 10.7 %fusion.25 = bf16[1024,3,64]{0,2,1:T(8,128)(2,1)S(1)} fusion(f32[3,1024,2048]{2,1,0:T(8,128)} %get-tuple-element.108, f32[3,1024]{1,0:T(4,128)S(1)} %fusion, f32[3,1024]{1,0:T(4,128)S(1)} %get-tuple-element.107, f32[1024,3,64]{0,2,1:T(8,128)S(1)} %bitcast.242, f32[1024,3,64]{0,2,1:T(8,128)S(1)} %bitcast.240, f32[3,64]{1,0:T(4,128)S(1)} %add.264), kind=kOutput, calls=%fused_computation.68 | convolution fusion | flops 825556992 | bytes 27157248 | tf_op jit(solution)/shard_map/hqk,khe->qhe/dot_general | solution.py:179
  88.0 14.9 %collective-permute-done.4 = bf16[96,768]{1,0:T(8,128)(2,1)S(1)} collective-permute-done((bf16[96,768]{1,0:T(8,128)(2,1)S(1)}, bf16[96,768]{1,0:T(8,128)(2,1)S(1)}, u32[]{:S(2)}, u32[]{:S(2)}) %collective-permute-start.4) | collective-permute-done | bytes 147488 | tf_op jit(solution)/shard_map/ppermute | solution.py:43
  119.3 4.9 collective-permute-done.5
  125.6 6.5 %all-gather.9.cloned.1.call-done = bf16[768,768]{1,0:T(8,128)(2,1)} async-done(((bf16[96,768]{1,0:T(8,128)(2,1)}), bf16[768,768]{1,0:T(8,128)(2,1)}) %all-gather.9.cloned.1.call-update) | async-done | bytes 1179664 | tf_op jit(solution)/shard_map/all_gather | solution.py:149
  141.3 21.5 %all-gather.11.cloned.1.call-done = bf16[768,2,768]{2,0,1:T(8,128)(2,1)} async-done(((bf16[96,2,768]{2,0,1:T(8,128)(2,1)}), bf16[768,2,768]{2,0,1:T(8,128)(2,1)}) %all-gather.11.cloned.1.call-update) | async-done | bytes 2359312 | tf_op jit(solution)/shard_map/all_gather | solution.py:149
  168.7 19.7 %all-gather.13.cloned.1.call-done = bf16[768,768]{1,0:T(8,128)(2,1)} async-done(((bf16[96,768]{1,0:T(8,128)(2,1)}), bf16[768,768]{1,0:T(8,128)(2,1)}) %all-gather.13.cloned.1.call-update) | async-done | bytes 1179664 | tf_op jit(solution)/shard_map/all_gather | solution.py:149
  192.8 12.9 %multiply_convert_fusion.7 = (bf16[256,768]{1,0:T(8,128)(2,1)S(1)}, f32[256,768]{1,0:T(8,128)S(1)}, f32[256,768]{1,0:T(8,128)S(1)}) fusion(f32[256,768]{1,0:T(8,128)S(1)} %fusion.87, bf16[256,768]{1,0:T(8,128)(2,1)S(1)} %fusion.92, bf16[768,2,768]{2,0,1:T(8,128)(2,1)S(1)} %copy-done.7), kind=kOutput, calls=%fused_computation.168 | convolution fusion | flops 314966016 | bytes 4325376 | tf_op jit(solution)/shard_map/dot_general | solution.py:25
  210.5 9.5 %collective-permute-done.9 = bf16[256,768]{1,0:T(8,128)(2,1)S(1)} collective-permute-done((bf16[256,768]{1,0:T(8,128)(2,1)S(1)}, bf16[256,768]{1,0:T(8,128)(2,1)S(1)}, u32[]{:S(2)}, u32[]{:S(2)}) %collective-permute-start.9) | collective-permute-done | bytes 393248 | tf_op jit(solution)/shard_map/ppermute | solution.py:43
  226.6 5.8 %copy.64 = bf16[768,2304]{1,0:T(8,128)(2,1)} copy(bf16[768,2304]{0,1:T(8,128)(2,1)} %pad_maximum_fusion.1) | data formatting | bytes 7077888
  246.8 5.3 %collective-permute-done.10 = bf16[256,768]{1,0:T(8,128)(2,1)S(1)} collective-permute-done((bf16[256,768]{1,0:T(8,128)(2,1)S(1)}, bf16[256,768]{1,0:T(8,128)(2,1)S(1)}, u32[]{:S(2)}, u32[]{:S(2)}) %collective-permute-start.10) | collective-permute-done | bytes 393248 | tf_op jit(solution)/shard_map/ppermute | solution.py:43
  263.9 5.9 %copy.62 = bf16[768,2304]{1,0:T(8,128)(2,1)} copy(bf16[768,2304]{0,1:T(8,128)(2,1)} %pad_maximum_fusion) | data formatting | bytes 7077888
  272.4 20.0 %multiply_reduce_fusion = (f32[3,1024]{1,0:T(4,128)S(1)}, f32[3,1024,2048]{2,1,0:T(8,128)}) fusion(f32[3,1024,2048]{2,1,0:T(8,128)} %get-tuple-element.108, f32[3,1024]{1,0:T(4,128)S(1)} %log_add_fusion, bf16[1024,3,64]{0,2,1:T(8,128)(2,1)S(1)} %reshape.250, f32[1024,3,64]{0,2,1:T(8,128)S(1)} %bitcast.243, f32[1024,3,64]{0,2,1:T(8,128)S(1)} %bitcast.241, ...), kind=kOutput, calls=%fused_computation.1 | convolution fusion | flops 825357312 | bytes 52323072 | tf_op jit(solution)/shard_map/qhe,khe->hqk/dot_general | solution.py:259
  292.4 17.8 %multiply_convert_fusion = bf16[3,1024,2048]{2,1,0:T(8,128)(2,1)S(1)} fusion(f32[3,1024,2048]{2,1,0:T(8,128)} %get-tuple-element.119, f32[3,1024,2048]{2,1,0:T(8,128)} %get-tuple-element.108, f32[3,1024]{1,0:T(4,128)S(1)} %get-tuple-element.118, f32[3,1024]{1,0:T(4,128)S(1)} %log_add_fusion), kind=kLoop, calls=%fused_computation | loop fusion | flops 25165824 | bytes 62939136 | tf_op jit(solution)/shard_map/convert_element_type | solution.py:261
  310.2 4.6 copy-done.2
  317.1 10.3 %fusion.2 = f32[3,64,2048]{2,1,0:T(8,128)S(1)} fusion(bf16[1024,3,64]{0,2,1:T(8,128)(2,1)S(1)} %reshape.250, f32[3,1024,2048]{2,1,0:T(8,128)} %get-tuple-element.108, f32[3,1024]{1,0:T(4,128)S(1)} %log_add_fusion), kind=kOutput, calls=%fused_computation.8 | convolution fusion | flops 817889280 | bytes 27144192 | tf_op jit(solution)/shard_map/hqk,qhe->khe/dot_general | solution.py:264
  330.8 8.6 %convert_reduce_fusion.2 = (f32[3,64]{1,0:T(4,128)S(1)}, bf16[3,64,1024]{2,1,0:T(8,128)(2,1)S(1)}) fusion(bf16[3,1024,2048]{2,1,0:T(8,128)(2,1)} %copy-done.2, bf16[1024,3,64]{0,2,1:T(8,128)(2,1)S(1)} %bitcast.234, bf16[1024,3,64]{0,2,1:T(8,128)(2,1)S(1)} %bitcast.232), kind=kOutput, calls=%fused_computation.125 | convolution fusion | flops 807665472 | bytes 13763328 | tf_op jit(solution)/shard_map/hqk,khe->qhe/dot_general | solution.py:262
  361.7 18.2 %collective-permute-done.12 = bf16[2,256,768]{2,1,0:T(8,128)(2,1)} collective-permute-done((bf16[2,256,768]{2,1,0:T(8,128)(2,1)S(1)}, bf16[2,256,768]{2,1,0:T(8,128)(2,1)}, u32[]{:S(2)}, u32[]{:S(2)}) %collective-permute-start.12) | collective-permute-done | bytes 786464 | tf_op jit(solution)/shard_map/ppermute | solution.py:43
  387.0 25.6 %collective-permute-done.13 = bf16[256,768]{1,0:T(8,128)(2,1)S(1)} collective-permute-done((bf16[256,768]{1,0:T(8,128)(2,1)S(1)}, bf16[256,768]{1,0:T(8,128)(2,1)S(1)}, u32[]{:S(2)}, u32[]{:S(2)}) %collective-permute-start.13) | collective-permute-done | bytes 393248 | tf_op jit(solution)/shard_map/ppermute | solution.py:43
  414.0 15.6 %collective-permute-done.7 = bf16[256,768]{1,0:T(8,128)(2,1)} collective-permute-done((bf16[256,768]{1,0:T(8,128)(2,1)S(1)}, bf16[256,768]{1,0:T(8,128)(2,1)}, u32[]{:S(2)}, u32[]{:S(2)}) %collective-permute-start.7) | collective-permute-done | bytes 393248 | tf_op jit(solution)/shard_map/ppermute | solution.py:43
  435.4 12.1 %collective-permute-done.14 = bf16[256,768]{1,0:T(8,128)(2,1)S(1)} collective-permute-done((bf16[256,768]{1,0:T(8,128)(2,1)S(1)}, bf16[256,768]{1,0:T(8,128)(2,1)S(1)}, u32[]{:S(2)}, u32[]{:S(2)}) %collective-permute-start.14) | collective-permute-done | bytes 393248 | tf_op jit(solution)/shard_map/ppermute | solution.py:43
  456.3 19.4 %reduce-scatter.11.cloned.1.call-done = f32[96,192]{0,1:T(8,128)} async-done(((f32[96,768]{0,1:T(8,128)}), f32[96,192]{0,1:T(8,128)}) %reduce-scatter.11.cloned.1.call-update) | async-done | bytes 73744 | tf_op jit(solution)/shard_map/reduce_scatter | solution.py:283
  (387 shorter events, 193.1 us)
Async XLA Ops:
  7.2 96.4 %all-gather.15.cloned.1.call-start = ((), (), s32[]{:S(2)}) async-start(), calls=%async_computation.11 | async-start | bytes 1671168 | tf_op jit(solution)/shard_map/all_gather | solution.py:140
  8.0 106.2 %all-gather.7.cloned.1.call-start = ((), (), s32[]{:S(2)}) async-start(), calls=%async_computation.6 | async-start | bytes 2654208 | tf_op jit(solution)/shard_map/all_gather | solution.py:149
  9.8 122.3 %all-gather.9.cloned.1.call-start = ((), (), s32[]{:S(2)}) async-start(), calls=%async_computation.7 | async-start | bytes 1327104 | tf_op jit(solution)/shard_map/all_gather | solution.py:149
  11.5 151.3 %all-gather.11.cloned.1.call-start = ((), (), s32[]{:S(2)}) async-start(), calls=%async_computation.8 | async-start | bytes 2654208 | tf_op jit(solution)/shard_map/all_gather | solution.py:149
  11.5 19.0 %collective-permute-start.3 = (bf16[96,2,768]{2,0,1:T(8,128)(2,1)}, bf16[96,2,768]{2,0,1:T(8,128)(2,1)}, u32[]{:S(2)}, u32[]{:S(2)}) collective-permute-start(bf16[96,2,768]{2,0,1:T(8,128)(2,1)} %copy.68), channel_id=1, source_target_pairs={{0,2},{1,3},{2,0},{3,1},{4,6},{5,7},{6,4},{7,5},{8,10},{9,11},{10,... | collective-permute-start | bytes 884744 | tf_op jit(solution)/shard_map/ppermute | solution.py:43
  17.1 22.8 %collective-permute-start.2 = (bf16[1024,768]{1,0:T(8,128)(2,1)S(1)}, bf16[1024,768]{1,0:T(8,128)(2,1)}, u32[]{:S(2)}, u32[]{:S(2)}) collective-permute-start(bf16[1024,768]{1,0:T(8,128)(2,1)S(1)} %bitcast.218), channel_id=1, source_target_pairs={{0,4},{4,0},{1,5},{5,1},{2,6},{6,2},{3,7},{7,3},{8,12},{12,8},{9,1... | collective-permute-start | bytes 4718600 | tf_op jit(solution)/shard_map/ppermute | solution.py:43
  81.3 30.1 %all-to-all-start = ((bf16[4,256,192]{1,2,0:T(8,128)(2,1)}), bf16[4,256,192]{1,2,0:T(8,128)(2,1)S(1)}, u32[]{:S(2)}, u32[]{:S(2)}) async-start(bf16[4,256,192]{1,2,0:T(8,128)(2,1)} %copy.45), calls=%async_computation | async-start | bytes 786432 | tf_op jit(solution)/shard_map/all_to_all | solution.py:183
  84.8 103.6 %all-gather.13.cloned.1.call-start = ((), (), s32[]{:S(2)}) async-start(), calls=%async_computation.9 | async-start | bytes 1327104 | tf_op jit(solution)/shard_map/all_gather | solution.py:149
  85.1 17.8 %collective-permute-start.4 = (bf16[96,768]{1,0:T(8,128)(2,1)S(1)}, bf16[96,768]{1,0:T(8,128)(2,1)S(1)}, u32[]{:S(2)}, u32[]{:S(2)}) collective-permute-start(bf16[96,768]{1,0:T(8,128)(2,1)S(1)} %copy-done.71), channel_id=1, source_target_pairs={{0,2},{1,3},{2,0},{3,1},{4,6},{5,7},{6,4},{7,5},{8,10},{9,11},{10,... | collective-permute-start | bytes 442376 | tf_op jit(solution)/shard_map/ppermute | solution.py:43
  103.6 327.6 %reduce-scatter.15.cloned.1.call-start = ((), (), s32[]{:S(2)}) async-start(), calls=%async_computation.13 | async-start | bytes 3981312 | tf_op jit(solution)/shard_map/reduce_scatter | solution.py:235
  190.7 15.0 %collective-permute-start.6 = (bf16[256,768]{1,0:T(8,128)(2,1)S(1)}, bf16[256,768]{1,0:T(8,128)(2,1)S(1)}, u32[]{:S(2)}, u32[]{:S(2)}) collective-permute-start(bf16[256,768]{1,0:T(8,128)(2,1)S(1)} %fusion.21), channel_id=1, source_target_pairs={{0,1},{1,0},{2,3},{3,2},{4,5},{5,4},{6,7},{7,6},{8,9},{9,8},{10,11... | collective-permute-start | bytes 1179656 | tf_op jit(solution)/shard_map/ppermute | solution.py:43
  255.9 14.0 %all-to-all-start.1 = ((bf16[256,4,192]{0,2,1:T(8,128)(2,1)}), bf16[256,4,192]{0,2,1:T(8,128)(2,1)S(1)}, u32[]{:S(2)}, u32[]{:S(2)}) async-start(bf16[256,4,192]{0,2,1:T(8,128)(2,1)} %bitcast.40), calls=%async_computation.1 | async-start | bytes 786432 | tf_op jit(solution)/shard_map/all_to_all | solution.py:253
  259.6 189.6 %reduce-scatter.13.cloned.1.call-start = ((), (), s32[]{:S(2)}) async-start(), calls=%async_computation.12 | async-start | bytes 3981312
  269.9 180.7 %reduce-scatter.17.cloned.1.call-start = ((), (), s32[]{:S(2)}) async-start(), calls=%async_computation.14 | async-start | bytes 2433024
  353.4 122.3 %reduce-scatter.11.cloned.1.call-start = ((), (), s32[]{:S(2)}) async-start(), calls=%async_computation.10 | async-start | bytes 491520 | tf_op jit(solution)/shard_map/reduce_scatter | solution.py:283
  359.7 20.3 %collective-permute-start.12 = (bf16[2,256,768]{2,1,0:T(8,128)(2,1)S(1)}, bf16[2,256,768]{2,1,0:T(8,128)(2,1)}, u32[]{:S(2)}, u32[]{:S(2)}) collective-permute-start(bf16[2,256,768]{2,1,0:T(8,128)(2,1)S(1)} %fusion.39), channel_id=1, source_target_pairs={{0,1},{1,0},{2,3},{3,2},{4,5},{5,4},{6,7},{7,6},{8,9},{9,8},{10,11... | collective-permute-start | bytes 2359304 | tf_op jit(solution)/shard_map/ppermute | solution.py:43
  382.9 29.7 %collective-permute-start.13 = (bf16[256,768]{1,0:T(8,128)(2,1)S(1)}, bf16[256,768]{1,0:T(8,128)(2,1)S(1)}, u32[]{:S(2)}, u32[]{:S(2)}) collective-permute-start(bf16[256,768]{1,0:T(8,128)(2,1)S(1)} %fusion.93), channel_id=1, source_target_pairs={{0,2},{1,3},{2,0},{3,1},{4,6},{5,7},{6,4},{7,5},{8,10},{9,11},{10,... | collective-permute-start | bytes 1179656 | tf_op jit(solution)/shard_map/ppermute | solution.py:43
  385.6 44.0 %collective-permute-start.7 = (bf16[256,768]{1,0:T(8,128)(2,1)S(1)}, bf16[256,768]{1,0:T(8,128)(2,1)}, u32[]{:S(2)}, u32[]{:S(2)}) collective-permute-start(bf16[256,768]{1,0:T(8,128)(2,1)S(1)} %copy-done.52), channel_id=1, source_target_pairs={{0,2},{1,3},{2,0},{3,1},{4,6},{5,7},{6,4},{7,5},{8,10},{9,11},{10,... | collective-permute-start | bytes 1179656 | tf_op jit(solution)/shard_map/ppermute | solution.py:43
  413.9 33.5 %collective-permute-start.14 = (bf16[256,768]{1,0:T(8,128)(2,1)S(1)}, bf16[256,768]{1,0:T(8,128)(2,1)S(1)}, u32[]{:S(2)}, u32[]{:S(2)}) collective-permute-start(bf16[256,768]{1,0:T(8,128)(2,1)S(1)} %get-tuple-element.96), channel_id=1, source_target_pairs={{0,2},{1,3},{2,0},{3,1},{4,6},{5,7},{6,4},{7,5},{8,10},{9,11},{10,... | collective-permute-start | bytes 1179656 | tf_op jit(solution)/shard_map/ppermute | solution.py:43
  431.2 24.6 %collective-permute-start.16 = (bf16[96,2304]{1,0:T(8,128)(2,1)}, bf16[96,2304]{1,0:T(8,128)(2,1)S(1)}, u32[]{:S(2)}, u32[]{:S(2)}) collective-permute-start(bf16[96,2304]{1,0:T(8,128)(2,1)} %reduce-scatter.15.cloned.1.call-done), channel_id=1, source_target_pairs={{0,2},{1,3},{2,0},{3,1},{4,6},{5,7},{6,4},{7,5},{8,10},{9,11},{10,... | collective-permute-start | bytes 1327112 | tf_op jit(solution)/shard_map/ppermute | solution.py:43
  432.3 52.3 %collective-permute-start.8 = (bf16[2,256,768]{2,1,0:T(8,128)(2,1)}, bf16[2,256,768]{2,1,0:T(8,128)(2,1)}, u32[]{:S(2)}, u32[]{:S(2)}) collective-permute-start(bf16[2,256,768]{2,1,0:T(8,128)(2,1)} %pad_maximum_fusion.8), channel_id=1, source_target_pairs={{0,1},{1,0},{2,3},{3,2},{4,5},{5,4},{6,7},{7,6},{8,9},{9,8},{10,11... | collective-permute-start | bytes 2359304 | tf_op jit(solution)/shard_map/ppermute | solution.py:43
  435.3 43.0 %collective-permute-start.19 = (f32[8,768]{1,0:T(8,128)S(1)}, f32[8,768]{1,0:T(8,128)S(1)}, u32[]{:S(2)}, u32[]{:S(2)}) collective-permute-start(f32[8,768]{1,0:T(8,128)S(1)} %add.314), channel_id=1, source_target_pairs={{0,1},{1,0},{2,3},{3,2},{4,5},{5,4},{6,7},{7,6},{8,9},{9,8},{10,11... | collective-permute-start | bytes 73736 | tf_op jit(solution)/shard_map/ppermute | solution.py:43
  449.2 42.9 %collective-permute-start.15 = (bf16[2,256,768]{2,1,0:T(8,128)(2,1)}, bf16[2,256,768]{2,1,0:T(8,128)(2,1)}, u32[]{:S(2)}, u32[]{:S(2)}) collective-permute-start(bf16[2,256,768]{2,1,0:T(8,128)(2,1)} %pad_maximum_fusion.9), channel_id=1, source_target_pairs={{0,1},{1,0},{2,3},{3,2},{4,5},{5,4},{6,7},{7,6},{8,9},{9,8},{10,11... | collective-permute-start | bytes 2359304 | tf_op jit(solution)/shard_map/ppermute | solution.py:43
  478.3 17.2 %collective-permute-start.17 = (f32[96,3072]{1,0:T(8,128)}, f32[96,3072]{1,0:T(8,128)}, u32[]{:S(2)}, u32[]{:S(2)}) collective-permute-start(f32[96,3072]{1,0:T(8,128)} %copy.55), channel_id=1, source_target_pairs={{0,4},{4,0},{1,5},{5,1},{2,6},{6,2},{3,7},{7,3},{8,12},{12,8},{9,1... | collective-permute-start | bytes 3538952 | tf_op jit(solution)/shard_map/ppermute | solution.py:43
  (99 other events, 617.8 us)
Sparse Core Ops, SparseCore 0:
  10.9 64.6 all-gather.14
  78.1 27.5 all-gather.6
  108.1 23.9 all-gather.8
  133.9 28.8 all-gather.10
  164.5 23.9 all-gather.12
  232.5 47.0 reduce-scatter.14
  283.1 47.9 reduce-scatter.12
  353.6 41.9 reduce-scatter.16
  452.8 22.9 reduce-scatter.10

commit v2 on v1

--- a/solution.py
+++ b/solution.py
@@ -1,6 +1,10 @@
+import functools
+
 import jax
 import jax.numpy as jnp
 from jax import lax
+from jax.experimental import pallas as pl
+from jax.experimental.pallas import tpu as pltpu
 from jax.sharding import PartitionSpec as P
 
 HEADS = 12
@@ -9,6 +13,7 @@
 norm_eps = 1e-05
 f32 = jnp.float32
 bf16 = jnp.bfloat16
+FAR = 1e32
 
 
 def layer_norm(inputs, norm_gain, norm_shift):
@@ -31,6 +36,178 @@
 
 def mm_tn(left, right):
     return lax.dot_general(left, right, (((0,), (0,)), ((), ())), preferred_element_type=f32)
+
+
+def head_lanes(x, h):
+    lane = lax.broadcasted_iota(jnp.int32, x.shape, 1)
+    return jnp.where((lane >= h * DH) & (lane < (h + 1) * DH), x, jnp.zeros_like(x))
+
+
+def distance_block(ints, start, n_keys, q_start, n_queries, span):
+    key = start + lax.broadcasted_iota(jnp.int32, (n_keys, 1), 0)
+    own, other = ints[0] * span, (1 - ints[0]) * span
+    key = jnp.where(key < span, key + own, key - span + other)
+    query = q_start + own + lax.broadcasted_iota(jnp.int32, (1, n_queries), 1)
+    valid = key < ints[1]
+    key_f = jnp.where(valid, key.astype(f32), FAR)
+    return jnp.abs(key_f - query.astype(f32))
+
+
+def attend_kernel(ints, slopes, q_ref, k_ref, vt_ref, o_ref, lse_ref, *, heads, chunk, span):
+    block = q_ref.shape[0]
+    q_start = pl.program_id(0) * block
+    q = q_ref[...] * SCALE
+    masked = [head_lanes(q, h) for h in range(heads)]
+
+    def step(i, carry):
+        start = pl.multiple_of(i * chunk, chunk)
+        distance = distance_block(ints, start, chunk, q_start, block, span)
+        keys = k_ref[pl.ds(start, chunk), :]
+        out = []
+        for h in range(heads):
+            top, total, acc = carry[h]
+            s = mm_nt(keys, masked[h]) - slopes[h] * distance
+            new_top = jnp.maximum(top, jnp.max(s, axis=0, keepdims=True))
+            p = jnp.exp(s - new_top)
+            fade = jnp.exp(top - new_top)
+            total = total * fade + jnp.sum(p, axis=0, keepdims=True)
+            vt = vt_ref[h * DH : (h + 1) * DH, pl.ds(start, chunk)]
+            acc = acc * fade + mm(vt, p.astype(bf16))
+            out.append((new_top, total, acc))
+        return tuple(out)
+
+    init = tuple(
+        (
+            jnp.full((1, block), -3e38, f32),
+            jnp.zeros((1, block), f32),
+            jnp.zeros((DH, block), f32),
+        )
+        for _ in range(heads)
+    )
+    done = lax.fori_loop(0, k_ref.shape[0] // chunk, step, init)
+    acc = jnp.concatenate([a / l for _, l, a in done], axis=0)
+    o_ref[...] = acc.T.astype(bf16)
+    lse = jnp.concatenate([m + jnp.log(l) for m, l, _ in done], axis=0)
+    pad = lse_ref.shape[0] - heads
+    lse_ref[...] = jnp.concatenate([lse, jnp.zeros((pad, block), f32)], axis=0)
+
+
+def attend_back_kernel(
+    ints, slopes, q_ref, k_ref, v_ref, kt_ref, lse_ref, o_ref, g_ref, dq_ref, dkv_ref, dqt,
+    *, heads, chunk, span
+):
+    block = q_ref.shape[0]
+    q_start = pl.program_id(0) * block
+    q = q_ref[...] * SCALE
+    g = g_ref[...]
+    q_of = [head_lanes(q, h) for h in range(heads)]
+    g_of = [head_lanes(g, h) for h in range(heads)]
+    weighted = (g.astype(f32) * o_ref[...].astype(f32)).T
+    row_dot = [
+        jnp.sum(weighted[h * DH : (h + 1) * DH], axis=0, keepdims=True) for h in range(heads)
+    ]
+    lse = [lse_ref[h : h + 1, :] for h in range(heads)]
+    q_all = jnp.concatenate(q_of, axis=0)
+    g_all = jnp.concatenate(g_of, axis=0)
+    dqt[...] = jnp.zeros_like(dqt)
+
+    @pl.when(pl.program_id(0) == 0)
+    def _():
+        dkv_ref[...] = jnp.zeros_like(dkv_ref)
+
+    per_half = span // chunk
+
+    def step(i, carry):
+        start = pl.multiple_of(i * chunk, chunk)
+        distance = distance_block(ints, start, chunk, q_start, block, span)
+        keys = k_ref[pl.ds(start, chunk), :]
+        values = v_ref[pl.ds(start, chunk), :]
+        probs, grads = [], []
+        for h in range(heads):
+            s = mm_nt(keys, q_of[h]) - slopes[h] * distance
+            p = jnp.exp(s - lse[h])
+            gp = mm_nt(values, g_of[h])
+            ds = (p * (gp - row_dot[h])).astype(bf16)
+            rows = slice(h * DH, (h + 1) * DH)
+            dqt[rows, :] += mm(kt_ref[rows, pl.ds(start, chunk)], ds)
+            probs.append(p.astype(bf16))
+            grads.append(ds)
+        half = i // per_half
+        at = pl.ds(pl.multiple_of((i % per_half) * chunk, chunk), chunk)
+        dkv_ref[half, 0, at, :] += mm(jnp.concatenate(grads, axis=1), q_all)
+        dkv_ref[half, 1, at, :] += mm(jnp.concatenate(probs, axis=1), g_all)
+        return carry
+
+    lax.fori_loop(0, k_ref.shape[0] // chunk, step, 0)
+    dq_ref[...] = (dqt[...] * SCALE).T.astype(bf16)
+
+
+def attention_forward(ints, slopes, q, k, vt, heads):
+    rows, part = q.shape
+    keys = k.shape[0]
+    block, chunk = min(256, rows), min(512, rows)
+    pairs = heads * rows * keys
+    return pl.pallas_call(
+        functools.partial(attend_kernel, heads=heads, chunk=chunk, span=rows),
+        grid_spec=pltpu.PrefetchScalarGridSpec(
+            num_scalar_prefetch=2,
+            grid=(rows // block,),
+            in_specs=[
+                pl.BlockSpec((block, part), lambda i, *_: (i, 0)),
+                pl.BlockSpec((keys, part), lambda i, *_: (0, 0)),
+                pl.BlockSpec((part, keys), lambda i, *_: (0, 0)),
+            ],
+            out_specs=[
+                pl.BlockSpec((block, part), lambda i, *_: (i, 0)),
+                pl.BlockSpec((8, block), lambda i, *_: (0, i)),
+            ],
+        ),
+        out_shape=[
+            jax.ShapeDtypeStruct((rows, part), bf16),
+            jax.ShapeDtypeStruct((8, rows), f32),
+        ],
+        cost_estimate=pl.CostEstimate(
+            flops=8 * pairs * DH, bytes_accessed=4 * keys * part, transcendentals=pairs
+        ),
+        name="attend",
+    )(ints, slopes, q, k, vt)
+
+
+def attention_backward(ints, slopes, q, k, v, kt, lse, o, g, heads):
+    rows, part = q.shape
+    keys = k.shape[0]
+    block, chunk = min(256, rows), min(512, rows)
+    pairs = heads * rows * keys
+    row_spec = pl.BlockSpec((block, part), lambda i, *_: (i, 0))
+    return pl.pallas_call(
+        functools.partial(attend_back_kernel, heads=heads, chunk=chunk, span=rows),
+        grid_spec=pltpu.PrefetchScalarGridSpec(
+            num_scalar_prefetch=2,
+            grid=(rows // block,),
+            in_specs=[
+                row_spec,
+                pl.BlockSpec((keys, part), lambda i, *_: (0, 0)),
+                pl.BlockSpec((keys, part), lambda i, *_: (0, 0)),
+                pl.BlockSpec((part, keys), lambda i, *_: (0, 0)),
+                pl.BlockSpec((8, block), lambda i, *_: (0, i)),
+                row_spec,
+                row_spec,
+            ],
+            out_specs=[
+                row_spec,
+                pl.BlockSpec((keys // rows, 2, rows, part), lambda i, *_: (0, 0, 0, 0)),
+            ],
+            scratch_shapes=[pltpu.VMEM((part, block), f32)],
+        ),
+        out_shape=[
+            jax.ShapeDtypeStruct((rows, part), bf16),
+            jax.ShapeDtypeStruct((keys // rows, 2, rows, part), f32),
+        ],
+        cost_estimate=pl.CostEstimate(
+            flops=30 * pairs * DH, bytes_accessed=16 * keys * part, transcendentals=pairs
+        ),
+        name="attend_back",
+    )(ints, slopes, q, k, v, kt, lse, o, g)
 
 
 def log2_of(n):
@@ -65,6 +242,10 @@
     for p, part in enumerate(held):
         out = lax.dynamic_update_index_in_dim(out, part, me ^ table[core, p], 0)
     return out
+
+
+def pair_up(mine, theirs, high):
+    return jnp.stack([jnp.where(high == 0, mine, theirs), jnp.where(high == 0, theirs, mine)])
 
 
 def sum_all(x, mesh_shape):
@@ -137,48 +318,33 @@
         qkv = gather_wshard(jnp.transpose(qkv_weight, (1, 0, 2)), n_ws, n_ctx)
         qkv = jnp.transpose(qkv, (1, 0, 2, 3)).reshape(3, width, part)
 
-        out_blocks = lax.all_gather(out_weight, ("wshard", "tp"), axis=0, tiled=False)
+        def own_half(weight):
+            return lax.dynamic_slice_in_dim(weight, c * half_rows, half_rows, 1)
+
+        ffn_half = own_half(
+            jnp.concatenate([jnp.transpose(gated_weight, (1, 0, 2)), down_weight[None]], axis=0)
+        )
+        ffn_far = swap(ffn_half, "tp", 2, n_tp)
+
+        def gather_half(half):
+            return lax.all_gather(half, ("wshard", "ctx"), axis=1, tiled=True)
+
+        ffn = [gather_half(ffn_half), gather_half(ffn_far)]
+
+        two = pair_up(out_weight, swap(out_weight, "tp", 1, n_tp), t % 2)
+        four = pair_up(two, swap(two, "tp", 2, n_tp), t // 2)
+        full_out = gather_wshard(four, n_ws, n_ctx)
         full_out = jnp.transpose(
-            out_blocks.reshape(n_ws, n_tp, shard_rows, part), (0, 2, 1, 3)
+            full_out.reshape(n_ws, n_tp, shard_rows, part), (0, 2, 1, 3)
         ).reshape(width, n_tp * part)
-
-        def own_half(weight):
-            return lax.dynamic_slice_in_dim(weight, c * half_rows, half_rows, 0)
-
-        def gather_half(half):
-            return lax.all_gather(half, ("wshard", "ctx"), axis=0, tiled=True)
-
-        gated_half, down_half = own_half(gated_weight), own_half(down_weight)
-        gated_far, down_far = swap(gated_half, "tp", 2, n_tp), swap(down_half, "tp", 2, n_tp)
-        gated = [gather_half(gated_half), gather_half(gated_far)]
-        down = [gather_half(down_half), gather_half(down_far)]
 
         q = (mm(x, qkv[0]) + qv_bias[0]).astype(bf16)
         keys = jnp.concatenate([mm(x, qkv[1]), mm(x_other, qkv[1])], axis=0).astype(bf16)
         values = (
             jnp.concatenate([mm(x, qkv[2]), mm(x_other, qkv[2])], axis=0) + qv_bias[1]
         ).astype(bf16)
-        local_pos = jnp.arange(length_here, dtype=jnp.int32)
-        q_pos = c * length_here + local_pos
-        k_pos = jnp.concatenate([q_pos, (1 - c) * length_here + local_pos])
-        qh = q.reshape(length_here, heads, DH)
-        kh = keys.reshape(n_ctx * length_here, heads, DH)
-        vh = values.reshape(n_ctx * length_here, heads, DH)
-
-        def scores_of():
-            raw = jnp.einsum("qhe,khe->hqk", qh, kh, preferred_element_type=f32) * SCALE
-            distance = jnp.abs(q_pos[:, None] - k_pos[None, :]).astype(f32)
-            biased = raw - slopes[:, None, None] * distance[None]
-            return jnp.where((k_pos < length)[None, None, :], biased, -1e30)
-
-        scores = scores_of()
-        row_top = jnp.max(scores, axis=-1, keepdims=True)
-        exponent = jnp.exp(scores - row_top)
-        row_total = jnp.sum(exponent, axis=-1, keepdims=True)
-        probs_low = (exponent / row_total).astype(bf16)
-        mixed = jnp.einsum("hqk,khe->qhe", probs_low, vh, preferred_element_type=f32)
-        mixed = mixed.astype(bf16).reshape(length_here, part)
-        log_total = (row_top + jnp.log(row_total))[:, :, 0]
+        ints = jnp.stack([c.astype(jnp.int32), length])
+        mixed, lse = attention_forward(ints, slopes, q, keys, values.T, heads)
 
         mixed_rows = lax.all_to_all(mixed, "tp", 0, 1, tiled=True)
         x_rows = lax.dynamic_slice_in_dim(x, t * rows, rows, 0).astype(f32)
@@ -192,12 +358,12 @@
 
         def forward(rows_low):
             kept, acts, total = [], [], None
-            for g, d in zip(gated, down):
-                gate, up = mm(rows_low, g[:, 0]), mm(rows_low, g[:, 1])
+            for wts in ffn:
+                gate, up = mm(rows_low, wts[0]), mm(rows_low, wts[1])
                 act = gated_unit(gate, up).astype(bf16)
                 kept.append((gate, up))
                 acts.append(act)
-                piece = mm_nt(act, d)
+                piece = mm_nt(act, wts[2])
                 total = piece if total is None else total + piece
             return kept, acts, total
 
@@ -214,13 +380,13 @@
 
         def backward(grad_low, kept):
             pieces, total = [], None
-            for g, d, (gate, up) in zip(gated, down, kept):
-                grad_act = mm(grad_low, d)
+            for wts, (gate, up) in zip(ffn, kept):
+                grad_act = mm(grad_low, wts[2])
                 unused, pull = jax.vjp(gated_unit, gate, up)
                 grad_gate, grad_up = pull(grad_act)
                 grad_gate, grad_up = grad_gate.astype(bf16), grad_up.astype(bf16)
                 pieces.append((grad_gate, grad_up))
-                piece = mm_nt(grad_gate, g[:, 0]) + mm_nt(grad_up, g[:, 1])
+                piece = mm_nt(grad_gate, wts[0]) + mm_nt(grad_up, wts[1])
                 total = piece if total is None else total + piece
             return pieces, total
 
@@ -234,16 +400,17 @@
         def reduce_rows(v):
             return lax.psum_scatter(v, ("wshard", "ctx"), scatter_dimension=0, tiled=True)
 
-        ffn_shards = []
-        for k in (1, 0):
+        def ffn_grads(k):
             gg = jnp.concatenate([ggu_own[k][0], ggu_near[k][0]], axis=0)
             gu = jnp.concatenate([ggu_own[k][1], ggu_near[k][1]], axis=0)
             act = jnp.concatenate([acts_own[k], acts_near[k]], axis=0)
-            whole = jnp.concatenate(
-                [mm_tn(norm_both, gg), mm_tn(norm_both, gu), mm_tn(grad_both, act)], axis=1
-            ).astype(bf16)
-            ffn_shards.append(reduce_rows(whole))
-        ffn_shard = ffn_shards[1].astype(f32) + swap(ffn_shards[0], "tp", 2, n_tp).astype(f32)
+            return [
+                mm_tn(norm_both, gg).astype(bf16),
+                mm_tn(norm_both, gu).astype(bf16),
+                mm_tn(grad_both, act).astype(bf16),
+            ]
+
+        far_shard = reduce_rows(jnp.concatenate(ffn_grads(1), axis=1))
 
         grad_norm1 = grad_pre2 + (back_own + back_got)
         unused, pull1 = jax.vjp(layer_norm, pre1, ln1_gain, ln1_bias)
@@ -252,42 +419,35 @@
         grad_mixed_rows = mm(grad_attn, full_out).astype(bf16)
         grad_mixed = lax.all_to_all(grad_mixed_rows, "tp", 1, 0, tiled=True)
         outw_part = mm_tn(grad_attn, mixed_rows).astype(bf16)
+        own_shard = reduce_rows(jnp.concatenate(ffn_grads(0) + [outw_part], axis=1))
+        hidden = gated_weight.shape[2]
+        ffn_shard = own_shard[:, : 3 * hidden].astype(f32) + swap(far_shard, "tp", 2, n_tp).astype(
+            f32
+        )
+        outw_cols = own_shard[:, 3 * hidden :].astype(f32).reshape(half_rows, n_tp, part)
+        outw_shard = tp_scatter(
+            jnp.transpose(outw_cols, (1, 0, 2)).reshape(n_tp * half_rows, part), t
+        )
         layer_output = tp_gather(output_rows, t)
 
-        gh = grad_mixed.reshape(length_here, heads, DH)
-        attention = jnp.exp(scores_of() - log_total[:, :, None])
-        grad_weights = jnp.einsum("qhe,khe->hqk", gh, vh, preferred_element_type=f32)
-        row_dot = jnp.sum(grad_weights * attention, axis=-1, keepdims=True)
-        grad_scores = (attention * (grad_weights - row_dot)).astype(bf16)
-        grad_q = jnp.einsum("hqk,khe->qhe", grad_scores, kh, preferred_element_type=f32) * SCALE
-        grad_k = jnp.einsum("hqk,qhe->khe", grad_scores, qh, preferred_element_type=f32) * SCALE
-        grad_v = jnp.einsum(
-            "hqk,qhe->khe", attention.astype(bf16), gh, preferred_element_type=f32
-        )
-        grad_q = grad_q.astype(bf16).reshape(length_here, part)
-        grad_kv = jnp.concatenate(
-            [grad_k.reshape(-1, part), grad_v.reshape(-1, part)], axis=1
-        )
-        grad_kv = grad_kv[:length_here] + swap(grad_kv[length_here:], "ctx", 1, n_ctx)
-        grad_kv = grad_kv.astype(bf16)
-        grad_k, grad_v = grad_kv[:, :part], grad_kv[:, part:]
+        grad_q, grad_kv = attention_backward(
+            ints, slopes, q, keys, values, keys.T, lse, mixed, grad_mixed, heads
+        )
+        grad_kv = (grad_kv[0] + swap(grad_kv[1], "ctx", 1, n_ctx)).astype(bf16)
+        grad_k, grad_v = grad_kv[0], grad_kv[1]
 
         input_part = mm_nt(grad_q, qkv[0]) + mm_nt(grad_k, qkv[1]) + mm_nt(grad_v, qkv[2])
         input_rows = grad_pre1 + tp_scatter(input_part, t)
         input_grad = tp_gather(input_rows.astype(bf16), t).astype(f32)
 
         grad_proj = jnp.concatenate([grad_q, grad_k, grad_v], axis=1)
-        qkv_out = jnp.concatenate([mm_tn(x, grad_proj).astype(bf16), outw_part], axis=1)
-        qkv_out = reduce_rows(qkv_out).astype(f32)
-        qkv_shard, outw_shard = qkv_out[:, : 3 * part], qkv_out[:, 3 * part :]
-        outw_shard = lax.psum_scatter(outw_shard, "tp", scatter_dimension=1, tiled=True)
+        qkv_shard = reduce_rows(mm_tn(x, grad_proj).astype(bf16)).astype(f32)
 
         shard = jnp.concatenate([ffn_shard, qkv_shard, outw_shard], axis=1)
         other = swap(shard, "ctx", 1, n_ctx)
         shard = jnp.concatenate(
             [jnp.where(c == 0, shard, other), jnp.where(c == 0, other, shard)], axis=0
         )
-        hidden = gated_weight.shape[2]
         gated_grad = shard[:, : 2 * hidden].reshape(shard_rows, 2, hidden)
         down_grad = shard[:, 2 * hidden : 3 * hidden]
         qkv_grad = shard[:, 3 * hidden : 3 * hidden + 3 * part].reshape(shard_rows, 3, part)

time: 521 us -> 455 us (0.87)
  matrix products: 139 us -> 45.7 us
  Pallas kernels: 0 us -> 54.2 us
  waiting for transfers between devices: 187 us -> 150 us
  other arithmetic: 58.8 us -> 37.1 us
  blocking collectives: 0 us -> 13.7 us
  local copies, waits for them, and re-layouts: 74.1 us -> 83.7 us
  starting transfers between devices: 33.2 us -> 42.6 us
    dot_general x6 -> x0, matrix products: 65.5 us -> none  [the longest x1 20 us: local(): jnp.einsum('qhe,khe->hqk', gh, vh, preferred_element_type=f32)]
    pallas_call x0 -> x2, Pallas kernels: none -> 54.2 us  [the longest x1 31.9 us: attention_backward(): pl.pallas_call(functools.partial(attend_back_kernel, heads=heads, chunk=c...]
    all_gather x5 -> x2, waiting for transfers between devices: 47.7 us -> 0.01 us  [gather_half(): return lax.all_gather(half, ('wshard', 'ctx'), axis=1, tiled=True)]
    reduce_scatter x1 -> x2, waiting for transfers between devices: 0.02 us -> 41.8 us  [reduce_rows(): lax.psum_scatter(v, ('wshard', 'ctx'), scatter_dimension=0, tiled=True)]
    convert_element_type x3, other arithmetic: 24.2 us -> 3.12 us  [the longest x1 1.81 us: local(): grad_kv = (grad_kv[0] + swap(grad_kv[1], 'ctx', 1, n_ctx)).astype(bf16)]
    reduce_scatter x1 -> x0, waiting for transfers between devices: 19.4 us -> none  [local(): lax.psum_scatter(outw_shard, 'tp', scatter_dimension=1, tiled=True)]
    dot_general x18, matrix products: 40.2 us -> 26.2 us  [mm(): lax.dot_general(left, right, (((1,), (0,)), ((), ())), preferred_element_...]
    all_to_all x0 -> x1, blocking collectives: none -> 13.7 us  [local(): grad_mixed = lax.all_to_all(grad_mixed_rows, 'tp', 1, 0, tiled=True)]
  transfers between devices with their start and end apart: 34 -> 34, of which waited for: 18 -> 17; matrix products, arithmetic and copies ran while one was open for 44% -> 26% of each run, Pallas kernels for 0% -> 5%
where the time goes in v2:
time: 455 us; the launch traced here: 446 us
  waiting for transfers between devices  150 us (33%)
  local copies, waits for them, and re-layouts  83.7 us (18%)
  Pallas kernels  54.2 us (12%)
  matrix products  45.7 us (10%)
  starting transfers between devices  42.6 us (9%)
  other arithmetic  37.1 us (8%)
  between operations  18.9 us (4%)
  blocking collectives  13.7 us (3%)
    ppermute x24, waiting for transfers between devices, swap(): return lax.ppermute(x, axis, [(i, i ^ mask) for i in range(n)])  107 us
    reduce_scatter x2, waiting for transfers between devices, reduce_rows(): lax.psum_scatter(v, ('wshard', 'ctx'), scatter_dimension=0, tiled=True)  41.8 us
    unnamed x182, local copies, waits for them, and re-layouts  34.9 us
    pallas_call x1, Pallas kernels, attention_backward(): pl.pallas_call(functools.partial(attend_back_kernel, heads=heads, chunk=c...  31.9 us
    ppermute x24, starting transfers between devices, swap(): return lax.ppermute(x, axis, [(i, i ^ mask) for i in range(n)])  31.5 us
    dot_general x18, matrix products, mm(): lax.dot_general(left, right, (((1,), (0,)), ((), ())), preferred_element_...  26.2 us
    pallas_call x1, Pallas kernels, attention_forward(): pl.pallas_call(functools.partial(attend_kernel, heads=heads, chunk=chunk,...  22.3 us
    all_to_all x1, blocking collectives, local(): grad_mixed = lax.all_to_all(grad_mixed_rows, 'tp', 1, 0, tiled=True)  13.7 us
  transfers between devices with their start and end apart: 34, of which 17 were waited for; matrix products, arithmetic and copies ran while one was open for 26% of the time, Pallas kernels for 5%

profile of v2, /device:TPU:0, one launch (start us, length us, event | category | flops | bytes accessed | tf_op | source)
XLA Modules:
  0.0 446.0 jit_solution(9882489775020051976)
XLA Ops:
  10.3 4.1 collective-permute-start.7
  21.6 4.6 %collective-permute-done.3 = bf16[192,192]{1,0:T(8,128)(2,1)S(1)} collective-permute-done((bf16[192,192]{1,0:T(8,128)(2,1)S(1)}, bf16[192,192]{1,0:T(8,128)(2,1)S(1)}, u32[]{:S(2)}, u32[]{:S(2)}) %collective-permute-start.3) | collective-permute-done | bytes 73760 | tf_op jit(solution)/shard_map/ppermute | solution.py:220
  32.5 10.4 %collective-permute-done.4 = bf16[2,192,192]{2,1,0:T(8,128)(2,1)} collective-permute-done((bf16[2,192,192]{2,1,0:T(8,128)(2,1)S(1)}, bf16[2,192,192]{2,1,0:T(8,128)(2,1)}, u32[]{:S(2)}, u32[]{:S(2)}) %collective-permute-start.4) | collective-permute-done | bytes 147488 | tf_op jit(solution)/shard_map/ppermute | solution.py:220
  77.4 22.3 %attend.1 = (bf16[1024,192]{1,0:T(8,128)(2,1)}, f32[8,1024]{1,0:T(8,128)}) custom-call(s32[2]{0:T(128)} %pad_add_fusion.ints, f32[3]{0:T(128)} %multiply_power_fusion.slopes, bf16[1024,192]{1,0:T(8,128)(2,1)} %fusion.20.q_ref, bf16[2048,192]{1,0:T(8,128)(2,1)} %copy.129.k_ref, bf16[192,2048]{1,0:T(8,128)(2,1)} %copy.130.vt_ref), custom_call_target="tpu_custom_call" | custom-call | flops 3221225472 | bytes 1572864 | tf_op jit(solution)/shard_map/attend/pallas_call | solution.py:150
  101.7 3.9 all-to-all-start
  109.0 5.3 %reshape.154 = bf16[4,4,192,192]{3,1,2,0:T(4,128)(2,1)} reshape(bf16[4,2,2,192,192]{4,2,1,3,0:T(2,128)(2,1)} %copy_dynamic-update-slice_fusion) | data formatting | bytes 2359296 | tf_op jit(solution)/shard_map/reshape | solution.py:338
  114.4 3.2 reshape.155
  124.4 4.6 %collective-permute-done.8 = bf16[256,768]{1,0:T(8,128)(2,1)S(1)} collective-permute-done((bf16[256,768]{1,0:T(8,128)(2,1)S(1)}, bf16[256,768]{1,0:T(8,128)(2,1)S(1)}, u32[]{:S(2)}, u32[]{:S(2)}) %collective-permute-start.8) | collective-permute-done | bytes 393248 | tf_op jit(solution)/shard_map/ppermute | solution.py:220
  131.0 3.0 multiply_convert_fusion.7
  135.2 3.0 multiply_convert_fusion.5
  142.3 3.4 multiply_convert_fusion.4
  150.9 3.2 collective-permute-done.9
  173.0 5.0 %collective-permute-done.13 = bf16[256,768]{1,0:T(8,128)(2,1)S(1)} collective-permute-done((bf16[256,768]{1,0:T(8,128)(2,1)S(1)}, bf16[256,768]{1,0:T(8,128)(2,1)S(1)}, u32[]{:S(2)}, u32[]{:S(2)}) %collective-permute-start.13) | collective-permute-done | bytes 393248 | tf_op jit(solution)/shard_map/ppermute | solution.py:220
  181.4 13.7 %all_to_all.38 = bf16[256,4,192]{0,2,1:T(8,128)(2,1)S(1)} all-to-all(bf16[256,4,192]{0,2,1:T(8,128)(2,1)S(1)} %bitcast.258), channel_id=1, replica_groups=mesh['wshard'=4,'ctx'=2,'tp'=4] {'tp'}, dimensions={1} | all-to-all | bytes 786432 | tf_op jit(solution)/shard_map/all_to_all | solution.py:420
  196.1 31.9 %attend_back.1 = (bf16[1024,192]{1,0:T(8,128)(2,1)}, f32[2,2,1024,192]{3,2,1,0:T(8,128)}) custom-call(s32[2]{0:T(128)} %pad_add_fusion.ints, f32[3]{0:T(128)} %multiply_power_fusion.slopes, bf16[1024,192]{1,0:T(8,128)(2,1)} %fusion.20.q_ref, bf16[2048,192]{1,0:T(8,128)(2,1)} %copy.129.k_ref, bf16[2048,192]{1,0:T(8,128)(2,1)} %fusion.v_ref, ...), custom_call_target="tpu_custom_call" | custom-call | flops 12079595520 | bytes 6291456 | tf_op jit(solution)/shard_map/attend_back/pallas_call | solution.py:182
  231.5 3.7 collective-permute-done.14
  248.3 4.0 copy.162
  260.2 6.7 %copy.160 = bf16[768,3072]{1,0:T(8,128)(2,1)} copy(bf16[768,3072]{0,1:T(8,128)(2,1)} %pad_maximum_fusion) | data formatting | bytes 9437184
  274.7 26.3 %collective-permute-done.15 = bf16[2,256,768]{2,1,0:T(8,128)(2,1)} collective-permute-done((bf16[2,256,768]{2,1,0:T(8,128)(2,1)S(1)}, bf16[2,256,768]{2,1,0:T(8,128)(2,1)}, u32[]{:S(2)}, u32[]{:S(2)}) %collective-permute-start.15) | collective-permute-done | bytes 786464 | tf_op jit(solution)/shard_map/ppermute | solution.py:220
  306.9 15.5 %collective-permute-done.16 = bf16[256,768]{1,0:T(8,128)(2,1)} collective-permute-done((bf16[256,768]{1,0:T(8,128)(2,1)}, bf16[256,768]{1,0:T(8,128)(2,1)}, u32[]{:S(2)}, u32[]{:S(2)}) %collective-permute-start.16) | collective-permute-done | bytes 393248 | tf_op jit(solution)/shard_map/ppermute | solution.py:220
  331.7 12.9 %collective-permute-done.17 = bf16[256,768]{1,0:T(8,128)(2,1)S(1)} collective-permute-done((bf16[256,768]{1,0:T(8,128)(2,1)}, bf16[256,768]{1,0:T(8,128)(2,1)S(1)}, u32[]{:S(2)}, u32[]{:S(2)}) %collective-permute-start.17) | collective-permute-done | bytes 393248 | tf_op jit(solution)/shard_map/ppermute | solution.py:220
  345.8 41.8 %reduce-scatter.10.cloned.1.call-done = bf16[96,3072]{1,0:T(8,128)(2,1)} async-done(((bf16[768,3072]{1,0:T(8,128)(2,1)}), bf16[96,3072]{1,0:T(8,128)(2,1)}) %reduce-scatter.10.cloned.1.call-update) | async-done | bytes 589840 | tf_op jit(solution)/shard_map/reduce_scatter | solution.py:401
  396.4 14.3 %collective-permute-done.21 = bf16[96,192]{1,0:T(8,128)(2,1)S(1)} collective-permute-done((bf16[96,192]{1,0:T(8,128)(2,1)S(1)}, bf16[96,192]{1,0:T(8,128)(2,1)S(1)}, u32[]{:S(2)}, u32[]{:S(2)}) %collective-permute-start.21) | collective-permute-done | bytes 36896 | tf_op jit(solution)/shard_map/ppermute | solution.py:220
  413.8 3.4 collective-permute-start.25
  (388 shorter events, 176.8 us)
Async XLA Ops:
  7.2 115.3 %all-gather.3.cloned.1.call-start = ((), (), s32[]{:S(2)}) async-start(), calls=%async_computation.5 | async-start | bytes 3981312 | tf_op jit(solution)/shard_map/all_gather | solution.py:330
  10.3 130.1 %all-gather.5.cloned.1.call-start = ((), (), s32[]{:S(2)}) async-start(), calls=%async_computation.6 | async-start | bytes 3981312 | tf_op jit(solution)/shard_map/all_gather | solution.py:330
  10.3 43.5 %collective-permute-start.7 = (bf16[3,96,768]{2,1,0:T(8,128)(2,1)}, bf16[3,96,768]{2,1,0:T(8,128)(2,1)}, u32[]{:S(2)}, u32[]{:S(2)}) collective-permute-start(bf16[3,96,768]{2,1,0:T(8,128)(2,1)} %fusion.93), channel_id=1, source_target_pairs={{0,2},{1,3},{2,0},{3,1},{4,6},{5,7},{6,4},{7,5},{8,10},{9,11},{10,... | collective-permute-start | bytes 1327112 | tf_op jit(solution)/shard_map/ppermute | solution.py:220
  14.4 11.8 %collective-permute-start.3 = (bf16[192,192]{1,0:T(8,128)(2,1)S(1)}, bf16[192,192]{1,0:T(8,128)(2,1)S(1)}, u32[]{:S(2)}, u32[]{:S(2)}) collective-permute-start(bf16[192,192]{1,0:T(8,128)(2,1)S(1)} %copy-done.72), channel_id=1, source_target_pairs={{0,1},{1,0},{2,3},{3,2},{4,5},{5,4},{6,7},{7,6},{8,9},{9,8},{10,11... | collective-permute-start | bytes 221192 | tf_op jit(solution)/shard_map/ppermute | solution.py:220
  16.0 29.5 %collective-permute-start = (bf16[1,3,192,192]{3,2,1,0:T(8,128)(2,1)}, bf16[1,3,192,192]{3,2,1,0:T(8,128)(2,1)}, u32[]{:S(2)}, u32[]{:S(2)}) collective-permute-start(bf16[1,3,192,192]{3,2,1,0:T(8,128)(2,1)} %bitcast.3), channel_id=1, source_target_pairs={{0,8},{4,20},{8,0},{12,28},{16,24},{20,4},{24,16},{28,12},{1,9},{5... | collective-permute-start | bytes 663560 | tf_op jit(solution)/shard_map/ppermute | solution.py:237
  17.5 51.8 %collective-permute-start.2 = (bf16[1024,768]{1,0:T(8,128)(2,1)S(1)}, bf16[1024,768]{1,0:T(8,128)(2,1)S(1)}, u32[]{:S(2)}, u32[]{:S(2)}) collective-permute-start(bf16[1024,768]{1,0:T(8,128)(2,1)S(1)} %bitcast.242), channel_id=1, source_target_pairs={{0,4},{4,0},{1,5},{5,1},{2,6},{6,2},{3,7},{7,3},{8,12},{12,8},{9,1... | collective-permute-start | bytes 4718600 | tf_op jit(solution)/shard_map/ppermute | solution.py:220
  26.3 16.5 %collective-permute-start.4 = (bf16[2,192,192]{2,1,0:T(8,128)(2,1)S(1)}, bf16[2,192,192]{2,1,0:T(8,128)(2,1)}, u32[]{:S(2)}, u32[]{:S(2)}) collective-permute-start(bf16[2,192,192]{2,1,0:T(8,128)(2,1)S(1)} %pad_maximum_fusion.16), channel_id=1, source_target_pairs={{0,2},{1,3},{2,0},{3,1},{4,6},{5,7},{6,4},{7,5},{8,10},{9,11},{10,... | collective-permute-start | bytes 442376 | tf_op jit(solution)/shard_map/ppermute | solution.py:220
  43.9 10.6 %collective-permute-start.5 = (bf16[1,2,2,192,192]{4,3,2,1,0:T(8,128)(2,1)S(1)}, bf16[1,2,2,192,192]{4,3,2,1,0:T(8,128)(2,1)}, u32[]{:S(2)}, u32[]{:S(2)}) collective-permute-start(bf16[1,2,2,192,192]{4,3,2,1,0:T(8,128)(2,1)S(1)} %maximum_bitcast_fusion), channel_id=1, source_target_pairs={{0,8},{4,20},{8,0},{12,28},{16,24},{20,4},{24,16},{28,12},{1,9},{5... | collective-permute-start | bytes 884744 | tf_op jit(solution)/shard_map/ppermute | solution.py:237
  47.5 13.7 %collective-permute-start.1 = (bf16[2,3,192,192]{3,2,1,0:T(8,128)(2,1)}, bf16[2,3,192,192]{3,2,1,0:T(8,128)(2,1)}, u32[]{:S(2)}, u32[]{:S(2)}) collective-permute-start(bf16[2,3,192,192]{3,2,1,0:T(8,128)(2,1)} %pad_maximum_fusion.12), channel_id=1, source_target_pairs={{0,16},{4,12},{8,24},{12,4},{16,0},{20,28},{24,8},{28,20},{1,17},{... | collective-permute-start | bytes 1327112 | tf_op jit(solution)/shard_map/ppermute | solution.py:237
  56.6 49.0 %collective-permute-start.6 = (bf16[2,2,2,192,192]{4,3,2,1,0:T(8,128)(2,1)}, bf16[2,2,2,192,192]{4,3,2,1,0:T(8,128)(2,1)}, u32[]{:S(2)}, u32[]{:S(2)}) collective-permute-start(bf16[2,2,2,192,192]{4,3,2,1,0:T(8,128)(2,1)} %pad_maximum_fusion.6), channel_id=1, source_target_pairs={{0,16},{4,12},{8,24},{12,4},{16,0},{20,28},{24,8},{28,20},{1,17},{... | collective-permute-start | bytes 1769480 | tf_op jit(solution)/shard_map/ppermute | solution.py:237
  101.7 15.9 %all-to-all-start = ((bf16[4,256,192]{1,2,0:T(8,128)(2,1)}), bf16[4,256,192]{1,2,0:T(8,128)(2,1)S(1)}, u32[]{:S(2)}, u32[]{:S(2)}) async-start(bf16[4,256,192]{1,2,0:T(8,128)(2,1)} %copy.131), calls=%async_computation | async-start | bytes 786432 | tf_op jit(solution)/shard_map/all_to_all | solution.py:349
  105.6 225.1 %reduce-scatter.14.cloned.1.call-start = ((), (), s32[]{:S(2)}) async-start(), calls=%async_computation.9 | async-start | bytes 1105920
  244.0 101.7 %reduce-scatter.12.cloned.1.call-start = ((), (), s32[]{:S(2)}) async-start(), calls=%async_computation.8 | async-start | bytes 3981312 | tf_op jit(solution)/shard_map/reduce_scatter | solution.py:401
  252.3 135.3 %reduce-scatter.10.cloned.1.call-start = ((), (), s32[]{:S(2)}) async-start(), calls=%async_computation.7 | async-start | bytes 5308416 | tf_op jit(solution)/shard_map/reduce_scatter | solution.py:401
  272.8 28.2 %collective-permute-start.15 = (bf16[2,256,768]{2,1,0:T(8,128)(2,1)S(1)}, bf16[2,256,768]{2,1,0:T(8,128)(2,1)}, u32[]{:S(2)}, u32[]{:S(2)}) collective-permute-start(bf16[2,256,768]{2,1,0:T(8,128)(2,1)S(1)} %fusion.33), channel_id=1, source_target_pairs={{0,1},{1,0},{2,3},{3,2},{4,5},{5,4},{6,7},{7,6},{8,9},{9,8},{10,11... | collective-permute-start | bytes 2359304 | tf_op jit(solution)/shard_map/ppermute | solution.py:220
  273.3 31.5 %collective-permute-start.10 = (bf16[256,768]{1,0:T(8,128)(2,1)}, bf16[256,768]{1,0:T(8,128)(2,1)}, u32[]{:S(2)}, u32[]{:S(2)}) collective-permute-start(bf16[256,768]{1,0:T(8,128)(2,1)} %get-tuple-element.128), channel_id=1, source_target_pairs={{0,2},{1,3},{2,0},{3,1},{4,6},{5,7},{6,4},{7,5},{8,10},{9,11},{10,... | collective-permute-start | bytes 1179656 | tf_op jit(solution)/shard_map/ppermute | solution.py:220
  303.6 18.8 %collective-permute-start.16 = (bf16[256,768]{1,0:T(8,128)(2,1)}, bf16[256,768]{1,0:T(8,128)(2,1)}, u32[]{:S(2)}, u32[]{:S(2)}) collective-permute-start(bf16[256,768]{1,0:T(8,128)(2,1)} %fusion.94), channel_id=1, source_target_pairs={{0,2},{1,3},{2,0},{3,1},{4,6},{5,7},{6,4},{7,5},{8,10},{9,11},{10,... | collective-permute-start | bytes 1179656 | tf_op jit(solution)/shard_map/ppermute | solution.py:220
  324.3 20.3 %collective-permute-start.17 = (bf16[256,768]{1,0:T(8,128)(2,1)}, bf16[256,768]{1,0:T(8,128)(2,1)S(1)}, u32[]{:S(2)}, u32[]{:S(2)}) collective-permute-start(bf16[256,768]{1,0:T(8,128)(2,1)} %get-tuple-element.132), channel_id=1, source_target_pairs={{0,2},{1,3},{2,0},{3,1},{4,6},{5,7},{6,4},{7,5},{8,10},{9,11},{10,... | collective-permute-start | bytes 1179656 | tf_op jit(solution)/shard_map/ppermute | solution.py:220
  327.1 93.4 %collective-permute-start.11 = (bf16[2,256,768]{2,1,0:T(8,128)(2,1)}, bf16[2,256,768]{2,1,0:T(8,128)(2,1)}, u32[]{:S(2)}, u32[]{:S(2)}) collective-permute-start(bf16[2,256,768]{2,1,0:T(8,128)(2,1)} %pad_maximum_fusion.7), channel_id=1, source_target_pairs={{0,1},{1,0},{2,3},{3,2},{4,5},{5,4},{6,7},{7,6},{8,9},{9,8},{10,11... | collective-permute-start | bytes 2359304 | tf_op jit(solution)/shard_map/ppermute | solution.py:220
  330.6 82.4 %collective-permute-start.24 = (f32[8,768]{1,0:T(8,128)}, f32[8,768]{1,0:T(8,128)}, u32[]{:S(2)}, u32[]{:S(2)}) collective-permute-start(f32[8,768]{1,0:T(8,128)} %add.306), channel_id=1, source_target_pairs={{0,1},{1,0},{2,3},{3,2},{4,5},{5,4},{6,7},{7,6},{8,9},{9,8},{10,11... | collective-permute-start | bytes 73736 | tf_op jit(solution)/shard_map/ppermute | solution.py:220
  345.8 46.3 %collective-permute-start.19 = (bf16[96,2304]{1,0:T(8,128)(2,1)}, bf16[96,2304]{1,0:T(8,128)(2,1)S(1)}, u32[]{:S(2)}, u32[]{:S(2)}) collective-permute-start(bf16[96,2304]{1,0:T(8,128)(2,1)} %reduce-scatter.12.cloned.1.call-done), channel_id=1, source_target_pairs={{0,2},{1,3},{2,0},{3,1},{4,6},{5,7},{6,4},{7,5},{8,10},{9,11},{10,... | collective-permute-start | bytes 1327112 | tf_op jit(solution)/shard_map/ppermute | solution.py:220
  391.5 36.5 %collective-permute-start.18 = (bf16[2,256,768]{2,1,0:T(8,128)(2,1)}, bf16[2,256,768]{2,1,0:T(8,128)(2,1)}, u32[]{:S(2)}, u32[]{:S(2)}) collective-permute-start(bf16[2,256,768]{2,1,0:T(8,128)(2,1)} %pad_maximum_fusion.8), channel_id=1, source_target_pairs={{0,1},{1,0},{2,3},{3,2},{4,5},{5,4},{6,7},{7,6},{8,9},{9,8},{10,11... | collective-permute-start | bytes 2359304 | tf_op jit(solution)/shard_map/ppermute | solution.py:220
  393.7 16.9 %collective-permute-start.21 = (bf16[96,192]{1,0:T(8,128)(2,1)S(1)}, bf16[96,192]{1,0:T(8,128)(2,1)S(1)}, u32[]{:S(2)}, u32[]{:S(2)}) collective-permute-start(bf16[96,192]{1,0:T(8,128)(2,1)S(1)} %fusion.96), channel_id=1, source_target_pairs={{0,2},{1,3},{2,0},{3,1},{4,6},{5,7},{6,4},{7,5},{8,10},{9,11},{10,... | collective-permute-start | bytes 110600 | tf_op jit(solution)/shard_map/ppermute | solution.py:220
  413.0 18.5 %collective-permute-start.22 = (f32[96,3072]{1,0:T(8,128)}, f32[96,3072]{1,0:T(8,128)}, u32[]{:S(2)}, u32[]{:S(2)}) collective-permute-start(f32[96,3072]{1,0:T(8,128)} %copy.150), channel_id=1, source_target_pairs={{0,4},{4,0},{1,5},{5,1},{2,6},{6,2},{3,7},{7,3},{8,12},{12,8},{9,1... | collective-permute-start | bytes 3538952 | tf_op jit(solution)/shard_map/ppermute | solution.py:220
  (97 other events, 702.9 us)
Sparse Core Ops, SparseCore 0:
  10.4 36.5 all-gather.2
  53.9 35.5 all-gather.4
  244.1 35.1 reduce-scatter.13
  282.6 47.8 reduce-scatter.11
  333.9 53.7 reduce-scatter.9
